TPU v7x, 32 devices: a whole 2x2x4 slice. The times are simulated.
32 devices in a mesh: gx: 4 (over x, core), gy: 8 (over z, y).
Axes of the slice: x: 2, y: 2, z: 4, core: 2. Of those that a mesh axis runs over, the one named last changes fastest.
Arguments:
- activation: bfloat16 [32, 16, 32, 128], P(None, 'gx', 'gy'), may hold values from -6 to 6
- out_grad: bfloat16 [32, 16, 32, 128], P(None, 'gx', 'gy'), may hold values from -6 to 6
- kernel: bfloat16 [3, 3, 3, 32, 32], replicated, may hold values from -0.21875 to 0.21875
Outputs:
- grad_input: bfloat16 [32, 16, 32, 128], P(None, 'gx', 'gy')
- grad_kernel: float32 [3, 3, 3, 32, 32], replicated
All inputs are finite; a program needn't handle non-finite values.
Results may differ from a plain program's by a relative error of at most 0.001.
Values may be sent and summed in bfloat16 or wider, within the bound.
No kernel may reach another device: no remote copies, remote signals or barrier semaphores. Data moves between devices by JAX's collectives and lax.ppermute only.
A program may use at most 64 MiB of HBM per device.

v0:
```python
import jax
import jax.numpy as jnp
from jax import lax
from jax.sharding import PartitionSpec as P


def extended(cells, sides, width):
    for axis, dim in sides:
        count = lax.axis_size(axis)
        ends = count - 1
        head = lax.slice_in_dim(cells, 0, width, axis=dim)
        tail = lax.slice_in_dim(cells, cells.shape[dim] - width, cells.shape[dim], axis=dim)
        cells = jnp.concatenate(
            [
                lax.ppermute(tail, axis, [(i, (i + 1) % count) for i in range(ends)]),
                cells,
                lax.ppermute(head, axis, [((i + 1) % count, i) for i in range(ends)]),
            ],
            axis=dim,
        )
    return cells


def padded_z(block):
    return jnp.pad(block, ((0, 0), (0, 0), (0, 0), (1, 1)))


def contract_cells(left, right):
    return lax.dot_general(
        left, right, (((1,), (1,)), ((), ())), preferred_element_type=jnp.float32
    )


def shards(activation, out_grad, kernel):
    channels = activation.shape[0]
    size_x, size_y, size_z = (activation.shape[1], activation.shape[2], activation.shape[3])
    cell_count = size_x * size_y * size_z
    grad_pad = padded_z(extended(out_grad, (("gx", 1), ("gy", 2)), 1))
    flat_act = activation.reshape(channels, cell_count)
    accumulated = jnp.zeros((channels, cell_count), jnp.float32)
    products = []
    for off_x in range(3):
        for off_y in range(3):
            for off_z in range(3):
                window = grad_pad[
                    :,
                    2 - off_x : 2 - off_x + size_x,
                    2 - off_y : 2 - off_y + size_y,
                    2 - off_z : 2 - off_z + size_z,
                ].reshape(channels, cell_count)
                accumulated = accumulated + jnp.dot(
                    kernel[off_x, off_y, off_z].T, window, preferred_element_type=jnp.float32
                )
                products.append(contract_cells(window, flat_act))
    grad_input = accumulated.reshape(channels, size_x, size_y, size_z).astype(jnp.bfloat16)
    local_terms = jnp.stack(products).reshape(3, 3, 3, channels, channels)
    summed = lax.psum(local_terms, ("gx", "gy"))
    total_cells = size_x * lax.axis_size("gx") * size_y * lax.axis_size("gy") * size_z
    grad_kernel = summed / jnp.sqrt(jnp.float32(total_cells))
    return (grad_input, grad_kernel)


def solution(mesh):
    return jax.shard_map(
        shards,
        mesh=mesh,
        in_specs=(P(None, "gx", "gy", None), P(None, "gx", "gy", None), P()),
        out_specs=(P(None, "gx", "gy", None), P()),
        check_vma=False,
    )
```

profile of v0, /device:TPU:8, one launch (start us, length us, event | category | flops | bytes accessed | tf_op | source)
XLA Modules:
  0.0 171.7 jit_solution(9164996284599008277)
XLA Ops:
  8.1 1.7 %collective-permute-start = (bf16[32,1,4,128]{3,0,2,1:T(8,128)(2,1)S(1)}, bf16[32,1,4,128]{3,0,2,1:T(8,128)(2,1)S(1)}, u32[]{:S(2)}, u32[]{:S(2)}) collective-permute-start(bf16[32,1,4,128]{3,0,2,1:T(8,128)(2,1)S(1)} %copy.183), channel_id=1, source_target_pairs={{0,8},{8,16},{16,24},{1,9},{9,17},{17,25},{2,10},{10,18},{18,26},{... | collective-permute-start | bytes 98312 | tf_op jit(solution)/shard_map/ppermute | solution.py:15
  9.9 1.3 collective-permute-start.1
  11.2 1.6 reshape.104
  12.9 1.3 collective-permute-done.1
  14.3 3.4 %collective-permute-start.2 = (bf16[32,6,1,128]{3,0,2,1:T(8,128)(2,1)S(1)}, bf16[32,6,1,128]{3,0,2,1:T(8,128)(2,1)S(1)}, u32[]{:S(2)}, u32[]{:S(2)}) collective-permute-start(bf16[32,6,1,128]{3,0,2,1:T(8,128)(2,1)S(1)} %get-tuple-element.29), channel_id=1, source_target_pairs={{0,1},{1,2},{2,3},{3,4},{4,5},{5,6},{6,7},{8,9},{9,10},{10,11},{11... | collective-permute-start | bytes 147464 | tf_op jit(solution)/shard_map/ppermute | solution.py:15
  17.7 3.3 %collective-permute-start.3 = (bf16[32,6,1,128]{3,0,2,1:T(8,128)(2,1)S(1)}, bf16[32,6,1,128]{3,0,2,1:T(8,128)(2,1)S(1)}, u32[]{:S(2)}, u32[]{:S(2)}) collective-permute-start(bf16[32,6,1,128]{3,0,2,1:T(8,128)(2,1)S(1)} %get-tuple-element.30), channel_id=1, source_target_pairs={{1,0},{2,1},{3,2},{4,3},{5,4},{6,5},{7,6},{9,8},{10,9},{11,10},{12... | collective-permute-start | bytes 147464 | tf_op jit(solution)/shard_map/ppermute | solution.py:17
  24.0 1.3 fusion.161
  53.3 1.1 convolution_bitcast_fusion.10
  55.2 1.0 reshape.110
  57.1 1.2 convolution_add_fusion.12
  58.3 1.0 convolution_add_fusion.11
  59.3 1.0 convolution_add_fusion.10
  60.3 1.0 convolution_add_fusion.9
  61.3 1.0 convolution_add_fusion.8
  62.3 1.0 convolution_add_fusion.7
  63.3 1.0 convolution_add_fusion.6
  64.3 1.0 convolution_add_fusion.5
  65.2 1.0 convolution_add_fusion.4
  66.2 1.0 convolution_add_fusion.3
  67.2 1.0 convolution_add_fusion.2
  68.2 1.0 fusion.13
  70.1 1.0 fusion.14
  71.9 91.1 %all-reduce.3.cloned.1.call-done = f32[3,3,3,32,32]{4,3,2,1,0:T(8,128)} async-done(((f32[3,3,3,32,32]{4,3,2,1,0:T(8,128)}), f32[3,3,3,32,32]{4,3,2,1,0:T(8,128)}) %all-reduce.3.cloned.1.call-update) | async-done | bytes 110608 | tf_op jit(solution)/shard_map/psum | solution.py:57
  163.0 1.8 %broadcast_multiply_fusion = f32[3,3,3,32,32]{4,3,2,1,0:T(8,128)} fusion(f32[3,3,3,32,32]{4,3,2,1,0:T(8,128)} %all-reduce.3.cloned.1.call-done), kind=kLoop, calls=%fused_computation.117 | loop fusion | flops 27648 | bytes 221184 | tf_op jit(solution)/shard_map/div | solution.py:59
  (150 shorter events, 35.1 us)
Async XLA Ops:
  7.2 18.1 %copy-start = (bf16[32,4,4,128]{3,2,1,0:T(4,128)(2,1)S(1)}, bf16[32,4,4,128]{3,2,1,0:T(4,128)(2,1)}, u32[]{:S(2)}) copy-start(bf16[32,4,4,128]{3,2,1,0:T(4,128)(2,1)} %param.3) | copy-start | bytes 393220
  7.2 5.6 %copy-start.1 = (bf16[32,4,4,128]{3,2,1,0:T(4,128)(2,1)S(1)}, bf16[32,4,4,128]{3,2,1,0:T(4,128)(2,1)}, u32[]{:S(2)}) copy-start(bf16[32,4,4,128]{3,2,1,0:T(4,128)(2,1)} %param.4) | copy-start | bytes 393220
  7.2 155.8 %all-reduce.3.cloned.1.call-start = ((), (), s32[]{:S(2)}) async-start(), calls=%async_computation | async-start | bytes 884736 | tf_op jit(solution)/shard_map/psum | solution.py:57
  8.1 4.7 %collective-permute-start = (bf16[32,1,4,128]{3,0,2,1:T(8,128)(2,1)S(1)}, bf16[32,1,4,128]{3,0,2,1:T(8,128)(2,1)S(1)}, u32[]{:S(2)}, u32[]{:S(2)}) collective-permute-start(bf16[32,1,4,128]{3,0,2,1:T(8,128)(2,1)S(1)} %copy.183), channel_id=1, source_target_pairs={{0,8},{8,16},{16,24},{1,9},{9,17},{17,25},{2,10},{10,18},{18,26},{... | collective-permute-start | bytes 98312 | tf_op jit(solution)/shard_map/ppermute | solution.py:15
  9.9 4.4 %collective-permute-start.1 = (bf16[32,1,4,128]{3,0,2,1:T(8,128)(2,1)S(1)}, bf16[32,1,4,128]{3,0,2,1:T(8,128)(2,1)S(1)}, u32[]{:S(2)}, u32[]{:S(2)}) collective-permute-start(bf16[32,1,4,128]{3,0,2,1:T(8,128)(2,1)S(1)} %copy.184), channel_id=1, source_target_pairs={{8,0},{16,8},{24,16},{9,1},{17,9},{25,17},{10,2},{18,10},{26,18},{... | collective-permute-start | bytes 98312 | tf_op jit(solution)/shard_map/ppermute | solution.py:17
  14.3 8.7 %collective-permute-start.2 = (bf16[32,6,1,128]{3,0,2,1:T(8,128)(2,1)S(1)}, bf16[32,6,1,128]{3,0,2,1:T(8,128)(2,1)S(1)}, u32[]{:S(2)}, u32[]{:S(2)}) collective-permute-start(bf16[32,6,1,128]{3,0,2,1:T(8,128)(2,1)S(1)} %get-tuple-element.29), channel_id=1, source_target_pairs={{0,1},{1,2},{2,3},{3,4},{4,5},{5,6},{6,7},{8,9},{9,10},{10,11},{11... | collective-permute-start | bytes 147464 | tf_op jit(solution)/shard_map/ppermute | solution.py:15
  17.7 6.0 %collective-permute-start.3 = (bf16[32,6,1,128]{3,0,2,1:T(8,128)(2,1)S(1)}, bf16[32,6,1,128]{3,0,2,1:T(8,128)(2,1)S(1)}, u32[]{:S(2)}, u32[]{:S(2)}) collective-permute-start(bf16[32,6,1,128]{3,0,2,1:T(8,128)(2,1)S(1)} %get-tuple-element.30), channel_id=1, source_target_pairs={{1,0},{2,1},{3,2},{4,3},{5,4},{6,5},{7,6},{9,8},{10,9},{11,10},{12... | collective-permute-start | bytes 147464 | tf_op jit(solution)/shard_map/ppermute | solution.py:17
  33.2 1.6 copy-start.3
  35.6 1.6 copy-start.7
  49.6 1.8 %copy-start.4 = (bf16[32,4,4,128]{3,0,2,1:T(8,128)(2,1)S(1)}, bf16[32,4,4,128]{3,0,2,1:T(8,128)(2,1)}, u32[]{:S(2)}) copy-start(bf16[32,4,4,128]{3,0,2,1:T(8,128)(2,1)} %get-tuple-element.26) | copy-start | bytes 393220
  50.7 1.8 %copy-start.2 = (bf16[32,4,4,128]{3,0,2,1:T(8,128)(2,1)S(1)}, bf16[32,4,4,128]{3,0,2,1:T(8,128)(2,1)}, u32[]{:S(2)}) copy-start(bf16[32,4,4,128]{3,0,2,1:T(8,128)(2,1)} %get-tuple-element.27) | copy-start | bytes 393220
  56.2 2.2 %copy-start.11 = (bf16[32,2048]{1,0:T(8,128)(2,1)S(1)}, bf16[32,2048]{1,0:T(8,128)(2,1)}, u32[]{:S(2)}) copy-start(bf16[32,2048]{1,0:T(8,128)(2,1)} %reshape.93) | copy-start | bytes 393220
  57.1 2.2 %copy-start.13 = (bf16[32,2048]{1,0:T(8,128)(2,1)S(1)}, bf16[32,2048]{1,0:T(8,128)(2,1)}, u32[]{:S(2)}) copy-start(bf16[32,2048]{1,0:T(8,128)(2,1)} %reshape.94) | copy-start | bytes 393220
  58.3 2.0 %copy-start.9 = (bf16[32,2048]{1,0:T(8,128)(2,1)S(1)}, bf16[32,2048]{1,0:T(8,128)(2,1)}, u32[]{:S(2)}) copy-start(bf16[32,2048]{1,0:T(8,128)(2,1)} %reshape.95) | copy-start | bytes 393220
  59.3 2.0 %copy-start.10 = (bf16[32,2048]{1,0:T(8,128)(2,1)S(1)}, bf16[32,2048]{1,0:T(8,128)(2,1)}, u32[]{:S(2)}) copy-start(bf16[32,2048]{1,0:T(8,128)(2,1)} %reshape.96) | copy-start | bytes 393220
  60.3 2.0 %copy-start.12 = (bf16[32,2048]{1,0:T(8,128)(2,1)S(1)}, bf16[32,2048]{1,0:T(8,128)(2,1)}, u32[]{:S(2)}) copy-start(bf16[32,2048]{1,0:T(8,128)(2,1)} %reshape.97) | copy-start | bytes 393220
  61.3 2.0 %copy-start.14 = (bf16[32,2048]{1,0:T(8,128)(2,1)S(1)}, bf16[32,2048]{1,0:T(8,128)(2,1)}, u32[]{:S(2)}) copy-start(bf16[32,2048]{1,0:T(8,128)(2,1)} %reshape.98) | copy-start | bytes 393220
  62.3 2.0 %copy-start.15 = (bf16[32,2048]{1,0:T(8,128)(2,1)S(1)}, bf16[32,2048]{1,0:T(8,128)(2,1)}, u32[]{:S(2)}) copy-start(bf16[32,2048]{1,0:T(8,128)(2,1)} %reshape.99) | copy-start | bytes 393220
  63.3 2.0 %copy-start.16 = (bf16[32,2048]{1,0:T(8,128)(2,1)S(1)}, bf16[32,2048]{1,0:T(8,128)(2,1)}, u32[]{:S(2)}) copy-start(bf16[32,2048]{1,0:T(8,128)(2,1)} %reshape.100) | copy-start | bytes 393220
  64.2 2.0 %copy-start.17 = (bf16[32,2048]{1,0:T(8,128)(2,1)S(1)}, bf16[32,2048]{1,0:T(8,128)(2,1)}, u32[]{:S(2)}) copy-start(bf16[32,2048]{1,0:T(8,128)(2,1)} %reshape.101) | copy-start | bytes 393220
  65.2 2.0 %copy-start.18 = (bf16[32,2048]{1,0:T(8,128)(2,1)S(1)}, bf16[32,2048]{1,0:T(8,128)(2,1)}, u32[]{:S(2)}) copy-start(bf16[32,2048]{1,0:T(8,128)(2,1)} %reshape.102) | copy-start | bytes 393220
  66.2 2.0 %copy-start.19 = (bf16[32,2048]{1,0:T(8,128)(2,1)S(1)}, bf16[32,2048]{1,0:T(8,128)(2,1)}, u32[]{:S(2)}) copy-start(bf16[32,2048]{1,0:T(8,128)(2,1)} %reshape.103) | copy-start | bytes 393220
  67.2 2.0 %copy-start.8 = (bf16[32,2048]{1,0:T(8,128)(2,1)S(1)}, bf16[32,2048]{1,0:T(8,128)(2,1)}, u32[]{:S(2)}) copy-start(bf16[32,2048]{1,0:T(8,128)(2,1)} %reshape.104) | copy-start | bytes 393220
  68.2 1.9 %copy-start.6 = (bf16[32,2048]{1,0:T(8,128)(2,1)S(1)}, bf16[32,2048]{1,0:T(8,128)(2,1)}, u32[]{:S(2)}) copy-start(bf16[32,2048]{1,0:T(8,128)(2,1)} %reshape.105) | copy-start | bytes 393220
  (2 other events, 2.4 us)
Sparse Core Ops, SparseCore 0:
  31.4 131.5 all-reduce.2
where the time goes:
time: 173 us; the launch traced here: 172 us
  waiting for transfers between devices  93.2 us (54%)
  matrix products  31 us (18%)
  local copies, waits for them, and re-layouts  19.9 us (12%)
  between operations  14.8 us (9%)
  starting transfers between devices  9.81 us (6%)
  other arithmetic  2.88 us (2%)
    psum x1, waiting for transfers between devices, shards(): summed = lax.psum(local_terms, ('gx', 'gy'))  91.1 us
    dot_general x27, matrix products, shards(): jnp.dot(kernel[off_x, off_y, off_z].T, window, preferred_element_type=jnp...  25.8 us
    reshape x27, local copies, waits for them, and re-layouts, shards(): window = grad_pad[:, 2 - off_x:2 - off_x + size_x, 2 - off_y:2 - off_y +...  13.6 us
    dot_general x27, matrix products, contract_cells(): lax.dot_general(left, right, (((1,), (1,)), ((), ())), preferred_element_...  5.22 us
    ppermute x2, starting transfers between devices, extended(): lax.ppermute(tail, axis, [(i, (i + 1) % count) for i in range(ends)])  5.17 us
    ppermute x2, starting transfers between devices, extended(): lax.ppermute(head, axis, [((i + 1) % count, i) for i in range(ends)])  4.61 us
    slice x29, local copies, waits for them, and re-layouts, shards(): grad_pad[:, 2 - off_x:2 - off_x + size_x, 2 - off_y:2 - off_y + size_y, 2...  3.73 us
  transfers between devices with their start and end apart: 5, of which 3 were waited for; matrix products, arithmetic and copies ran while one was open for 25% of the time, Pallas kernels for 0%

commit v1 on v0

v1 whole, which is shorter than its diff:
```python
import functools

import jax
import jax.numpy as jnp
from jax import lax
from jax.experimental import pallas as pl
from jax.experimental.pallas import tpu as pltpu
from jax.sharding import PartitionSpec as P

BOTH = ("gx", "gy")
VMEM = pl.BlockSpec(memory_space=pltpu.VMEM)
BF16, F32 = jnp.bfloat16, jnp.float32


def params():
    return pltpu.CompilerParams(vmem_limit_bytes=16 << 20)


def cost(flops, nbytes):
    return pl.CostEstimate(flops=flops, bytes_accessed=nbytes, transcendentals=0)


def pairs(counts, partner):
    nx, ny = counts
    flat = []
    for ix in range(nx):
        for iy in range(ny):
            jx, jy = partner(ix, iy)
            flat.append((ix * ny + iy, jx * ny + jy))
    return flat


def shift_z(cells, step):
    size = cells.shape[-1]
    lane = lax.broadcasted_iota(jnp.int32, cells.shape, cells.ndim - 1)
    moved = pltpu.roll(cells, step % size, cells.ndim - 1)
    return jnp.where(lane == (0 if step == 1 else size - 1), 0.0, moved)


def prepare_body(act_ref, grad_ref, act_out, grad_out, near_out, far_out):
    channels, size_x, size_y, size_z = grad_ref.shape
    right = lax.axis_index("gx") % 2 == 0
    for x in range(size_x):
        grad = jnp.swapaxes(grad_ref[:, x].astype(F32), 0, 1).astype(BF16)
        grad_out[x] = grad
    near_out[...] = grad_out[jnp.where(right, size_x - 1, 0)]
    far_out[...] = grad_out[jnp.where(right, 0, size_x - 1)]
    for x in range(size_x):
        act = jnp.swapaxes(act_ref[:, x].astype(F32), 0, 1)
        act_out[x, :, :channels] = shift_z(act, 1).astype(BF16)
        act_out[x, :, channels : 2 * channels] = act.astype(BF16)
        act_out[x, :, 2 * channels :] = shift_z(act, -1).astype(BF16)


def faces_body(grad_ref, near_ref, far_ref, left_out, right_out, near_out, far_out):
    size_x, size_y = grad_ref.shape[:2]
    ix, iy = lax.axis_index("gx"), lax.axis_index("gy")
    even = ix % 2 == 0
    zero = jnp.zeros(near_ref.shape, BF16)
    near, far = near_ref[...], far_ref[...]
    left = jnp.where(even, far, near)
    right = jnp.where(even, near, far)
    left_out[...] = jnp.where(ix == 0, zero, left)
    right_out[...] = jnp.where(ix == lax.axis_size("gx") - 1, zero, right)
    high = jnp.where(iy % 2 == 0, size_y - 1, 0)
    low = size_y - 1 - high
    for out, y in ((near_out, high), (far_out, low)):
        out[0] = left_out[y]
        out[size_x + 1] = right_out[y]
        for x in range(size_x):
            out[x + 1] = grad_ref[x, y]


def columns(grad_ref, left_ref, right_ref, near_ref, far_ref):
    size_x, size_y = grad_ref.shape[:2]
    iy = lax.axis_index("gy")
    even = iy % 2 == 0

    def column(x, y):
        if y < 0:
            face = jnp.where(even, far_ref[x + 1], near_ref[x + 1])
            return jnp.where(iy == 0, jnp.zeros_like(face), face)
        if y >= size_y:
            face = jnp.where(even, near_ref[x + 1], far_ref[x + 1])
            return jnp.where(iy == lax.axis_size("gy") - 1, jnp.zeros_like(face), face)
        if x < 0:
            return left_ref[y]
        if x >= size_x:
            return right_ref[y]
        return grad_ref[x, y]

    return column


def fill_halo(grad_ref, left_ref, right_ref, near_ref, far_ref, cells):
    size_x, size_y = grad_ref.shape[:2]
    column = columns(grad_ref, left_ref, right_ref, near_ref, far_ref)
    for x in range(-1, size_x + 1):
        for y in range(-1, size_y + 1):
            cells[x + 1, y + 1] = column(x, y)


def stacked(cells, x, y):
    return jnp.concatenate([cells[x - a + 2, y - b + 2] for a in range(3) for b in range(3)], axis=0)


def half_of():
    bits = lax.axis_index("gx") ^ (lax.axis_index("gy"))
    width = max(lax.axis_size("gx"), lax.axis_size("gy")).bit_length()
    parity = bits & 1
    for k in range(1, width):
        parity = parity ^ ((bits >> k) & 1)
    return parity


def weights_body(act_ref, grad_ref, left_ref, right_ref, near_ref, far_ref, send_out, keep_out, cells, total):
    size_x, size_y, rows3, size_z = act_ref.shape
    channels = rows3 // 3
    fill_halo(grad_ref, left_ref, right_ref, near_ref, far_ref, cells)
    acc = jnp.zeros((9 * channels, rows3), F32)
    for x in range(size_x):
        for y in range(0, size_y, 2):
            lhs = jnp.concatenate([stacked(cells, x, y), stacked(cells, x, y + 1)], axis=1)
            rhs = jnp.concatenate([act_ref[x, y], act_ref[x, y + 1]], axis=1)
            acc = acc + lax.dot_general(lhs, rhs, (((1,), (1,)), ((), ())), preferred_element_type=F32)
    rows = 9 * channels // 4
    spread = [acc[3 * rows :, k * channels : (k + 1) * channels] for k in range(3)]
    dense = jnp.concatenate([acc[: 3 * rows], jnp.concatenate(spread, axis=0)], axis=1)
    total[: 3 * rows] = dense
    half = total.shape[0] // 2
    total[3 * rows :] = jnp.zeros((total.shape[0] - 3 * rows, total.shape[1]), F32)
    mine = half_of()
    keep_out[...] = total[pl.ds(pl.multiple_of(mine * half, 8), half)]
    send_out[...] = total[pl.ds(pl.multiple_of((1 - mine) * half, 8), half)]


def finish_body(scale, mine_ref, other_ref, out_ref, total):
    channels = out_ref.shape[-1]
    half = mine_ref.shape[0]
    mine = half_of()
    total[pl.ds(pl.multiple_of(mine * half, 8), half)] = mine_ref[...] / scale
    total[pl.ds(pl.multiple_of((1 - mine) * half, 8), half)] = other_ref[...] / scale
    rows = 9 * channels // 4
    for ab in range(9):
        for c in range(3):
            first = ab * channels
            parts = []
            for r in range(first, first + channels, 8):
                if r < 3 * rows:
                    parts.append(total[r : r + 8, c * channels : (c + 1) * channels])
                else:
                    q = c * rows + r - 3 * rows
                    parts.append(total[q : q + 8, 3 * channels : 4 * channels])
            out_ref[ab // 3, ab % 3, c] = jnp.concatenate(parts, axis=0)


def inputs_body(grad_ref, left_ref, right_ref, near_ref, far_ref, kernel_ref, out_ref, cells):
    channels, size_x, size_y, size_z = out_ref.shape
    fill_halo(grad_ref, left_ref, right_ref, near_ref, far_ref, cells)
    taps = jnp.concatenate(
        [
            jnp.concatenate([kernel_ref[a, b, c] for a in range(3) for b in range(3)], axis=0).astype(F32)
            for c in range(3)
        ],
        axis=1,
    )
    taps = jnp.transpose(taps).astype(BF16)
    for x in range(size_x):
        rows = []
        for y in range(0, size_y, 2):
            rhs = jnp.concatenate([stacked(cells, x, y), stacked(cells, x, y + 1)], axis=1)
            terms = jnp.dot(taps, rhs, preferred_element_type=F32)
            for k in range(2):
                part = terms[:, k * size_z : (k + 1) * size_z]
                row = shift_z(part[:channels], -1) + part[channels : 2 * channels]
                rows.append(row + shift_z(part[2 * channels :], 1))
        out_ref[:, x] = jnp.swapaxes(jnp.stack(rows), 0, 1).astype(BF16)


def shards(activation, out_grad, kernel):
    channels, size_x, size_y, size_z = activation.shape
    counts = (lax.axis_size("gx"), lax.axis_size("gy"))
    nx, ny = counts
    shape = jax.ShapeDtypeStruct
    volume = channels * size_x * size_y * size_z

    def permute(value, partner):
        return lax.ppermute(value, BOTH, pairs(counts, partner))

    def odd_y(ix, iy):
        if iy in (0, ny - 1):
            return ix ^ 1, iy
        return ix, (iy + 1 if iy % 2 else iy - 1)

    def odd_x(ix, iy):
        return (ix + 1 if ix % 2 else ix - 1) % nx, iy

    face = shape((size_y, channels, size_z), BF16)
    long_face = shape((size_x + 2, channels, size_z), BF16)
    act, grad, near, far = pl.pallas_call(
        prepare_body,
        out_shape=(
            shape((size_x, size_y, 3 * channels, size_z), BF16),
            shape((size_x, size_y, channels, size_z), BF16),
            face,
            face,
        ),
        in_specs=[VMEM] * 2,
        out_specs=(VMEM,) * 4,
        compiler_params=params(),
        cost_estimate=cost(0, 12 * volume),
        name="prepare",
    )(activation, out_grad)
    far = permute(far, odd_x)
    near = permute(near, lambda ix, iy: (ix ^ 1, iy))
    left, right, near, far = pl.pallas_call(
        faces_body,
        out_shape=(face, face, long_face, long_face),
        in_specs=[VMEM] * 3,
        out_specs=(VMEM,) * 4,
        compiler_params=params(),
        cost_estimate=cost(0, 4 * volume),
        name="faces",
    )(grad, near, far)
    far = permute(far, odd_y)
    near = permute(near, lambda ix, iy: (ix, iy ^ 1))
    halo = [pltpu.VMEM((size_x + 2, size_y + 2, channels, size_z), BF16)]
    rows = (9 * 3 * channels * channels // 128 + 15) // 16 * 8
    half = shape((rows, 128), F32)
    send, total = pl.pallas_call(
        weights_body,
        out_shape=(half, half),
        in_specs=[VMEM] * 6,
        out_specs=(VMEM,) * 2,
        scratch_shapes=halo + [pltpu.VMEM((2 * rows, 128), F32)],
        compiler_params=params(),
        cost_estimate=cost(54 * channels * volume, 12 * volume),
        name="weights",
    )(act, grad, left, right, near, far)
    total = total + permute(send, lambda ix, iy: (ix ^ 1, iy))
    step = 2
    while step < nx:
        total = total + permute(total, lambda ix, iy: (ix ^ 1 ^ step, iy))
        step *= 2
    step = 1
    while step < ny:
        total = total + permute(total, lambda ix, iy: (ix ^ 1, iy ^ step))
        step *= 2
    grad_input = pl.pallas_call(
        inputs_body,
        out_shape=shape(activation.shape, BF16),
        in_specs=[VMEM] * 6,
        out_specs=VMEM,
        scratch_shapes=halo,
        compiler_params=params(),
        cost_estimate=cost(54 * channels * volume, 12 * volume),
        name="inputs",
    )(grad, left, right, near, far, kernel)
    other = permute(total, lambda ix, iy: (ix ^ 1, iy))
    cell_count = nx * size_x * ny * size_y * size_z
    grad_kernel = pl.pallas_call(
        functools.partial(finish_body, float(cell_count) ** 0.5),
        out_shape=shape(kernel.shape, F32),
        in_specs=[VMEM] * 2,
        out_specs=VMEM,
        scratch_shapes=[pltpu.VMEM((2 * rows, 128), F32)],
        compiler_params=params(),
        name="finish",
    )(total, other)
    return (grad_input, grad_kernel)


def solution(mesh):
    return jax.shard_map(
        shards,
        mesh=mesh,
        in_specs=(P(None, "gx", "gy", None), P(None, "gx", "gy", None), P()),
        out_specs=(P(None, "gx", "gy", None), P()),
        check_vma=False,
    )
```

time: 173 us -> 36.1 us (0.21)
  the two profiles are of different devices: /device:TPU:8 before, /device:TPU:25 now
where the time goes in v1:
time: 36.1 us; the launch traced here: 35.9 us
  waiting for transfers between devices  22.5 us (62%)
  starting transfers between devices  7.85 us (22%)
  Pallas kernels  3.08 us (9%)
  local copies, waits for them, and re-layouts  1.81 us (5%)
  between operations  0.68 us (2%)
    ppermute x10, waiting for transfers between devices, permute(): return lax.ppermute(value, BOTH, pairs(counts, partner))  22.5 us
    ppermute x10, starting transfers between devices, permute(): return lax.ppermute(value, BOTH, pairs(counts, partner))  7.85 us
    unnamed x6, local copies, waits for them, and re-layouts  1.81 us
    pallas_call x1, Pallas kernels, shards(): pl.pallas_call(inputs_body, out_shape=shape(activation.shape, BF16), in_s...  1.3 us
    pallas_call x1, Pallas kernels, shards(): pl.pallas_call(functools.partial(finish_body, float(cell_count) ** 0.5),...  0.94 us
  transfers between devices with their start and end apart: 10, of which 8 were waited for; matrix products, arithmetic and copies ran while one was open for 0% of the time, Pallas kernels for 4%

profile of v1, /device:TPU:25, one launch (start us, length us, event | category | flops | bytes accessed | tf_op | source)
XLA Modules:
  0.0 35.9 jit_solution(13360973924061777671)
XLA Ops:
  0.6 0.9 %copy-done.1 = bf16[32,4,4,128]{3,2,1,0:T(4,128)(2,1)S(1)} copy-done((bf16[32,4,4,128]{3,2,1,0:T(4,128)(2,1)S(1)}, bf16[32,4,4,128]{3,2,1,0:T(4,128)(2,1)}, u32[]{:S(2)}) %copy-start.1) | copy-done | bytes 131096
  1.5 0.9 %copy-done.2 = bf16[32,4,4,128]{3,2,1,0:T(4,128)(2,1)S(1)} copy-done((bf16[32,4,4,128]{3,2,1,0:T(4,128)(2,1)S(1)}, bf16[32,4,4,128]{3,2,1,0:T(4,128)(2,1)}, u32[]{:S(2)}) %copy-start.2) | copy-done | bytes 131096
  2.4 0.2 prepare.1
  2.6 0.7 %collective-permute-start = (bf16[4,32,128]{2,1,0:T(8,128)(2,1)S(1)}, bf16[4,32,128]{2,1,0:T(8,128)(2,1)S(1)}, u32[]{:S(2)}, u32[]{:S(2)}) collective-permute-start(bf16[4,32,128]{2,1,0:T(8,128)(2,1)S(1)} %get-tuple-element.13), channel_id=1, source_target_pairs={{0,8},{1,9},{2,10},{3,11},{4,12},{5,13},{6,14},{7,15},{8,0},{9,1},... | collective-permute-start | bytes 98312 | tf_op jit(solution)/shard_map/ppermute | solution.py:188
  3.4 1.2 %collective-permute-start.1 = (bf16[4,32,128]{2,1,0:T(8,128)(2,1)S(1)}, bf16[4,32,128]{2,1,0:T(8,128)(2,1)S(1)}, u32[]{:S(2)}, u32[]{:S(2)}) collective-permute-start(bf16[4,32,128]{2,1,0:T(8,128)(2,1)S(1)} %get-tuple-element.14), channel_id=1, source_target_pairs={{0,24},{1,25},{2,26},{3,27},{4,28},{5,29},{6,30},{7,31},{8,16},{9,... | collective-permute-start | bytes 98312 | tf_op jit(solution)/shard_map/ppermute | solution.py:188
  4.6 2.2 %collective-permute-done.1.far_ref = bf16[4,32,128]{2,1,0:T(8,128)(2,1)S(1)} collective-permute-done((bf16[4,32,128]{2,1,0:T(8,128)(2,1)S(1)}, bf16[4,32,128]{2,1,0:T(8,128)(2,1)S(1)}, u32[]{:S(2)}, u32[]{:S(2)}) %collective-permute-start.1) | collective-permute-done | bytes 32800 | tf_op jit(solution)/shard_map/ppermute | solution.py:188
  6.7 1.3 %collective-permute-start.2 = (bf16[6,32,128]{2,1,0:T(8,128)(2,1)S(1)}, bf16[6,32,128]{2,1,0:T(8,128)(2,1)S(1)}, u32[]{:S(2)}, u32[]{:S(2)}) collective-permute-start(bf16[6,32,128]{2,1,0:T(8,128)(2,1)S(1)} %get-tuple-element.17), channel_id=1, source_target_pairs={{0,1},{1,0},{2,3},{3,2},{4,5},{5,4},{6,7},{7,6},{8,9},{9,8},{10,11... | collective-permute-start | bytes 147464 | tf_op jit(solution)/shard_map/ppermute | solution.py:188
  8.1 0.1 collective-permute-start.3
  8.2 1.6 %collective-permute-done.2.near_ref = bf16[6,32,128]{2,1,0:T(8,128)(2,1)S(1)} collective-permute-done((bf16[6,32,128]{2,1,0:T(8,128)(2,1)S(1)}, bf16[6,32,128]{2,1,0:T(8,128)(2,1)S(1)}, u32[]{:S(2)}, u32[]{:S(2)}) %collective-permute-start.2) | collective-permute-done | bytes 49184 | tf_op jit(solution)/shard_map/ppermute | solution.py:188
  9.8 2.1 %collective-permute-done.3.far_ref = bf16[6,32,128]{2,1,0:T(8,128)(2,1)S(1)} collective-permute-done((bf16[6,32,128]{2,1,0:T(8,128)(2,1)S(1)}, bf16[6,32,128]{2,1,0:T(8,128)(2,1)S(1)}, u32[]{:S(2)}, u32[]{:S(2)}) %collective-permute-start.3) | collective-permute-done | bytes 49184 | tf_op jit(solution)/shard_map/ppermute | solution.py:188
  11.9 0.6 %weights.1 = (f32[112,128]{1,0:T(8,128)S(1)}, f32[112,128]{1,0:T(8,128)S(1)}) custom-call(bf16[4,4,96,128]{3,2,1,0:T(8,128)(2,1)S(1)} %get-tuple-element.19.act_ref, bf16[4,4,32,128]{3,2,1,0:T(8,128)(2,1)S(1)} %get-tuple-element.12.grad_ref, bf16[4,32,128]{2,1,0:T(8,128)(2,1)S(1)} %get-tuple-element.15.left_ref, ...), custom_call_target="tpu_custom_call" | custom-call | flops 113246208 | bytes 786432 | tf_op jit(solution)/shard_map/weights/pallas_call | solution.py:230
  12.5 1.6 %collective-permute-start.4 = (f32[112,128]{1,0:T(8,128)S(1)}, f32[112,128]{1,0:T(8,128)S(1)}, u32[]{:S(2)}, u32[]{:S(2)}) collective-permute-start(f32[112,128]{1,0:T(8,128)S(1)} %get-tuple-element.21), channel_id=1, source_target_pairs={{0,8},{1,9},{2,10},{3,11},{4,12},{5,13},{6,14},{7,15},{8,0},{9,1},... | collective-permute-start | bytes 172040 | tf_op jit(solution)/shard_map/ppermute | solution.py:188
  14.1 0.9 %collective-permute-done.4 = f32[112,128]{1,0:T(8,128)S(1)} collective-permute-done((f32[112,128]{1,0:T(8,128)S(1)}, f32[112,128]{1,0:T(8,128)S(1)}, u32[]{:S(2)}, u32[]{:S(2)}) %collective-permute-start.4) | collective-permute-done | bytes 57376 | tf_op jit(solution)/shard_map/ppermute | solution.py:188
  15.0 1.5 %collective-permute-start.5 = (f32[112,128]{1,0:T(8,128)S(1)}, f32[112,128]{1,0:T(8,128)S(1)}, u32[]{:S(2)}, u32[]{:S(2)}) collective-permute-start(f32[112,128]{1,0:T(8,128)S(1)} %add.15), channel_id=1, source_target_pairs={{0,24},{1,25},{2,26},{3,27},{4,28},{5,29},{6,30},{7,31},{8,16},{9,... | collective-permute-start | bytes 172040 | tf_op jit(solution)/shard_map/ppermute | solution.py:188
  16.5 2.4 %collective-permute-done.5 = f32[112,128]{1,0:T(8,128)S(1)} collective-permute-done((f32[112,128]{1,0:T(8,128)S(1)}, f32[112,128]{1,0:T(8,128)S(1)}, u32[]{:S(2)}, u32[]{:S(2)}) %collective-permute-start.5) | collective-permute-done | bytes 57376 | tf_op jit(solution)/shard_map/ppermute | solution.py:188
  19.0 0.1 collective-permute-start.6
  19.0 3.9 %collective-permute-done.6 = f32[112,128]{1,0:T(8,128)S(1)} collective-permute-done((f32[112,128]{1,0:T(8,128)S(1)}, f32[112,128]{1,0:T(8,128)S(1)}, u32[]{:S(2)}, u32[]{:S(2)}) %collective-permute-start.6) | collective-permute-done | bytes 57376 | tf_op jit(solution)/shard_map/ppermute | solution.py:188
  23.0 0.5 %collective-permute-start.7 = (f32[112,128]{1,0:T(8,128)S(1)}, f32[112,128]{1,0:T(8,128)S(1)}, u32[]{:S(2)}, u32[]{:S(2)}) collective-permute-start(f32[112,128]{1,0:T(8,128)S(1)} %add.17), channel_id=1, source_target_pairs={{0,10},{1,11},{2,8},{3,9},{4,14},{5,15},{6,12},{7,13},{8,2},{9,3},... | collective-permute-start | bytes 172040 | tf_op jit(solution)/shard_map/ppermute | solution.py:188
  23.5 3.5 %collective-permute-done.7 = f32[112,128]{1,0:T(8,128)S(1)} collective-permute-done((f32[112,128]{1,0:T(8,128)S(1)}, f32[112,128]{1,0:T(8,128)S(1)}, u32[]{:S(2)}, u32[]{:S(2)}) %collective-permute-start.7) | collective-permute-done | bytes 57376 | tf_op jit(solution)/shard_map/ppermute | solution.py:188
  26.9 0.4 %collective-permute-start.8 = (f32[112,128]{1,0:T(8,128)S(1)}, f32[112,128]{1,0:T(8,128)S(1)}, u32[]{:S(2)}, u32[]{:S(2)}) collective-permute-start(f32[112,128]{1,0:T(8,128)S(1)} %add.18), channel_id=1, source_target_pairs={{0,12},{1,13},{2,14},{3,15},{4,8},{5,9},{6,10},{7,11},{8,4},{9,5},... | collective-permute-start | bytes 172040 | tf_op jit(solution)/shard_map/ppermute | solution.py:188
  27.3 5.9 %collective-permute-done.8 = f32[112,128]{1,0:T(8,128)S(1)} collective-permute-done((f32[112,128]{1,0:T(8,128)S(1)}, f32[112,128]{1,0:T(8,128)S(1)}, u32[]{:S(2)}, u32[]{:S(2)}) %collective-permute-start.8) | collective-permute-done | bytes 57376 | tf_op jit(solution)/shard_map/ppermute | solution.py:188
  33.2 0.5 %collective-permute-start.9 = (f32[112,128]{1,0:T(8,128)S(1)}, f32[112,128]{1,0:T(8,128)S(1)}, u32[]{:S(2)}, u32[]{:S(2)}) collective-permute-start(f32[112,128]{1,0:T(8,128)S(1)} %add.19.mine_ref), channel_id=1, source_target_pairs={{0,8},{1,9},{2,10},{3,11},{4,12},{5,13},{6,14},{7,15},{8,0},{9,1},... | collective-permute-start | bytes 172040 | tf_op jit(solution)/shard_map/ppermute | solution.py:188
  33.7 1.3 %inputs.1 = bf16[32,4,4,128]{3,2,1,0:T(4,128)(2,1)} custom-call(bf16[4,4,32,128]{3,2,1,0:T(8,128)(2,1)S(1)} %get-tuple-element.12.grad_ref, bf16[4,32,128]{2,1,0:T(8,128)(2,1)S(1)} %get-tuple-element.15.left_ref, bf16[4,32,128]{2,1,0:T(8,128)(2,1)S(1)} %get-tuple-element.16.right_ref, bf16[6,32,128]{2,1,0:T(8,128)(2,1)S(1)} %collective-permute-done.2.near_ref, ...), custom_call_target="tpu_custom_call" | custom-call | flops 113246208 | bytes 786432 | tf_op jit(solution)/shard_map/inputs/pallas_call | solution.py:249
  35.0 0.9 %finish.1 = f32[3,3,3,32,32]{4,3,2,1,0:T(8,128)} custom-call(f32[112,128]{1,0:T(8,128)S(1)} %add.19.mine_ref, f32[112,128]{1,0:T(8,128)S(1)} %collective-permute-done.9.other_ref), custom_call_target="tpu_custom_call" | custom-call | tf_op jit(solution)/shard_map/finish/pallas_call | solution.py:261
  (12 shorter events, 0.1 us)
Async XLA Ops:
  0.6 0.9 %copy-start.1 = (bf16[32,4,4,128]{3,2,1,0:T(4,128)(2,1)S(1)}, bf16[32,4,4,128]{3,2,1,0:T(4,128)(2,1)}, u32[]{:S(2)}) copy-start(bf16[32,4,4,128]{3,2,1,0:T(4,128)(2,1)} %act_ref.1) | copy-start | bytes 393220
  1.5 0.9 %copy-start.2 = (bf16[32,4,4,128]{3,2,1,0:T(4,128)(2,1)S(1)}, bf16[32,4,4,128]{3,2,1,0:T(4,128)(2,1)}, u32[]{:S(2)}) copy-start(bf16[32,4,4,128]{3,2,1,0:T(4,128)(2,1)} %grad_ref.1) | copy-start | bytes 393220
  2.6 1.9 %collective-permute-start = (bf16[4,32,128]{2,1,0:T(8,128)(2,1)S(1)}, bf16[4,32,128]{2,1,0:T(8,128)(2,1)S(1)}, u32[]{:S(2)}, u32[]{:S(2)}) collective-permute-start(bf16[4,32,128]{2,1,0:T(8,128)(2,1)S(1)} %get-tuple-element.13), channel_id=1, source_target_pairs={{0,8},{1,9},{2,10},{3,11},{4,12},{5,13},{6,14},{7,15},{8,0},{9,1},... | collective-permute-start | bytes 98312 | tf_op jit(solution)/shard_map/ppermute | solution.py:188
  3.4 3.3 %collective-permute-start.1 = (bf16[4,32,128]{2,1,0:T(8,128)(2,1)S(1)}, bf16[4,32,128]{2,1,0:T(8,128)(2,1)S(1)}, u32[]{:S(2)}, u32[]{:S(2)}) collective-permute-start(bf16[4,32,128]{2,1,0:T(8,128)(2,1)S(1)} %get-tuple-element.14), channel_id=1, source_target_pairs={{0,24},{1,25},{2,26},{3,27},{4,28},{5,29},{6,30},{7,31},{8,16},{9,... | collective-permute-start | bytes 98312 | tf_op jit(solution)/shard_map/ppermute | solution.py:188
  6.7 3.0 %collective-permute-start.2 = (bf16[6,32,128]{2,1,0:T(8,128)(2,1)S(1)}, bf16[6,32,128]{2,1,0:T(8,128)(2,1)S(1)}, u32[]{:S(2)}, u32[]{:S(2)}) collective-permute-start(bf16[6,32,128]{2,1,0:T(8,128)(2,1)S(1)} %get-tuple-element.17), channel_id=1, source_target_pairs={{0,1},{1,0},{2,3},{3,2},{4,5},{5,4},{6,7},{7,6},{8,9},{9,8},{10,11... | collective-permute-start | bytes 147464 | tf_op jit(solution)/shard_map/ppermute | solution.py:188
  8.1 3.8 %collective-permute-start.3 = (bf16[6,32,128]{2,1,0:T(8,128)(2,1)S(1)}, bf16[6,32,128]{2,1,0:T(8,128)(2,1)S(1)}, u32[]{:S(2)}, u32[]{:S(2)}) collective-permute-start(bf16[6,32,128]{2,1,0:T(8,128)(2,1)S(1)} %get-tuple-element.18), channel_id=1, source_target_pairs={{0,8},{1,2},{2,1},{3,4},{4,3},{5,6},{6,5},{7,15},{8,0},{9,10},{10,... | collective-permute-start | bytes 147464 | tf_op jit(solution)/shard_map/ppermute | solution.py:188
  12.5 2.5 %collective-permute-start.4 = (f32[112,128]{1,0:T(8,128)S(1)}, f32[112,128]{1,0:T(8,128)S(1)}, u32[]{:S(2)}, u32[]{:S(2)}) collective-permute-start(f32[112,128]{1,0:T(8,128)S(1)} %get-tuple-element.21), channel_id=1, source_target_pairs={{0,8},{1,9},{2,10},{3,11},{4,12},{5,13},{6,14},{7,15},{8,0},{9,1},... | collective-permute-start | bytes 172040 | tf_op jit(solution)/shard_map/ppermute | solution.py:188
  15.0 3.9 %collective-permute-start.5 = (f32[112,128]{1,0:T(8,128)S(1)}, f32[112,128]{1,0:T(8,128)S(1)}, u32[]{:S(2)}, u32[]{:S(2)}) collective-permute-start(f32[112,128]{1,0:T(8,128)S(1)} %add.15), channel_id=1, source_target_pairs={{0,24},{1,25},{2,26},{3,27},{4,28},{5,29},{6,30},{7,31},{8,16},{9,... | collective-permute-start | bytes 172040 | tf_op jit(solution)/shard_map/ppermute | solution.py:188
  18.9 14.7 %copy-start = (bf16[3,3,3,32,32]{4,3,2,1,0:T(8,128)(2,1)S(1)}, bf16[3,3,3,32,32]{4,3,2,1,0:T(8,128)(2,1)}, u32[]{:S(2)}) copy-start(bf16[3,3,3,32,32]{4,3,2,1,0:T(8,128)(2,1)} %kernel_ref.1) | copy-start | bytes 165892
  19.0 4.0 %collective-permute-start.6 = (f32[112,128]{1,0:T(8,128)S(1)}, f32[112,128]{1,0:T(8,128)S(1)}, u32[]{:S(2)}, u32[]{:S(2)}) collective-permute-start(f32[112,128]{1,0:T(8,128)S(1)} %add.16), channel_id=1, source_target_pairs={{0,9},{1,8},{2,11},{3,10},{4,13},{5,12},{6,15},{7,14},{8,1},{9,0},... | collective-permute-start | bytes 172040 | tf_op jit(solution)/shard_map/ppermute | solution.py:188
  23.0 4.0 %collective-permute-start.7 = (f32[112,128]{1,0:T(8,128)S(1)}, f32[112,128]{1,0:T(8,128)S(1)}, u32[]{:S(2)}, u32[]{:S(2)}) collective-permute-start(f32[112,128]{1,0:T(8,128)S(1)} %add.17), channel_id=1, source_target_pairs={{0,10},{1,11},{2,8},{3,9},{4,14},{5,15},{6,12},{7,13},{8,2},{9,3},... | collective-permute-start | bytes 172040 | tf_op jit(solution)/shard_map/ppermute | solution.py:188
  26.9 6.3 %collective-permute-start.8 = (f32[112,128]{1,0:T(8,128)S(1)}, f32[112,128]{1,0:T(8,128)S(1)}, u32[]{:S(2)}, u32[]{:S(2)}) collective-permute-start(f32[112,128]{1,0:T(8,128)S(1)} %add.18), channel_id=1, source_target_pairs={{0,12},{1,13},{2,14},{3,15},{4,8},{5,9},{6,10},{7,11},{8,4},{9,5},... | collective-permute-start | bytes 172040 | tf_op jit(solution)/shard_map/ppermute | solution.py:188
  33.2 1.8 %collective-permute-start.9 = (f32[112,128]{1,0:T(8,128)S(1)}, f32[112,128]{1,0:T(8,128)S(1)}, u32[]{:S(2)}, u32[]{:S(2)}) collective-permute-start(f32[112,128]{1,0:T(8,128)S(1)} %add.19.mine_ref), channel_id=1, source_target_pairs={{0,8},{1,9},{2,10},{3,11},{4,12},{5,13},{6,14},{7,15},{8,0},{9,1},... | collective-permute-start | bytes 172040 | tf_op jit(solution)/shard_map/ppermute | solution.py:188

commit v2 on v1

v2 whole, which is shorter than its diff:
```python
import functools

import jax
import jax.numpy as jnp
from jax import lax
from jax.experimental import pallas as pl
from jax.experimental.pallas import tpu as pltpu
from jax.sharding import PartitionSpec as P

BOTH = ("gx", "gy")
VMEM = pl.BlockSpec(memory_space=pltpu.VMEM)
BF16, F32 = jnp.bfloat16, jnp.float32


def params(limit=16 << 20):
    return pltpu.CompilerParams(vmem_limit_bytes=limit)


def cost(flops, nbytes):
    return pl.CostEstimate(flops=flops, bytes_accessed=nbytes, transcendentals=0)


def pairs(counts, partner):
    nx, ny = counts
    flat = []
    for ix in range(nx):
        for iy in range(ny):
            jx, jy = partner(ix, iy)
            flat.append((ix * ny + iy, jx * ny + jy))
    return flat


def shift_z(cells, step):
    size = cells.shape[-1]
    lane = lax.broadcasted_iota(jnp.int32, cells.shape, cells.ndim - 1)
    moved = pltpu.roll(cells, step % size, cells.ndim - 1)
    return jnp.where(lane == (0 if step == 1 else size - 1), 0.0, moved)


def gradient_body(grad_hbm, grad_out, near_out, held, sems):
    size_x = grad_out.shape[0]
    copies = [pltpu.make_async_copy(grad_hbm.at[:, x], held.at[x], sems.at[x]) for x in range(size_x)]
    for copy in copies:
        copy.start()
    for x, copy in enumerate(copies):
        copy.wait()
        grad_out[x] = jnp.swapaxes(held[x].astype(F32), 0, 1).astype(BF16)
    near_out[...] = grad_out[jnp.where(lax.axis_index("gx") % 2 == 0, size_x - 1, 0)]


def activation_body(act_ref, act_out):
    channels, size_x = act_ref.shape[:2]
    for x in range(size_x):
        act = jnp.swapaxes(act_ref[:, x].astype(F32), 0, 1)
        act_out[x, :, :channels] = shift_z(act, 1).astype(BF16)
        act_out[x, :, channels : 2 * channels] = act.astype(BF16)
        act_out[x, :, 2 * channels :] = shift_z(act, -1).astype(BF16)


def faces_body(grad_ref, near_ref, even_out, odd_out):
    size_x, size_y = grad_ref.shape[:2]
    high = jnp.where(lax.axis_index("gy") % 2 == 0, size_y - 1, 0)
    for out, y in ((even_out, high), (odd_out, size_y - 1 - high)):
        for x in range(size_x):
            out[x] = grad_ref[x, y]
        out[size_x] = near_ref[y]


def half_of():
    bits = lax.axis_index("gx") ^ lax.axis_index("gy")
    width = max(lax.axis_size("gx"), lax.axis_size("gy")).bit_length()
    parity = bits & 1
    for k in range(1, width):
        parity = parity ^ ((bits >> k) & 1)
    return parity


def stacked(cells, x, y):
    return jnp.concatenate([cells[x - a + 2, y - b + 2] for a in range(3) for b in range(3)], axis=0)


def pack(terms, total):
    channels = terms.shape[1] // 3
    rows = 9 * channels // 4
    spread = [terms[3 * rows :, k * channels : (k + 1) * channels] for k in range(3)]
    total[: 3 * rows] = jnp.concatenate([terms[: 3 * rows], jnp.concatenate(spread, axis=0)], axis=1)
    total[3 * rows :] = jnp.zeros((total.shape[0] - 3 * rows, total.shape[1]), F32)


def split(total, send_out, keep_out):
    half = keep_out.shape[0]
    mine = half_of()
    keep_out[...] = total[pl.ds(pl.multiple_of(mine * half, 8), half)]
    send_out[...] = total[pl.ds(pl.multiple_of((1 - mine) * half, 8), half)]


def weights_body(act_ref, grad_ref, near_ref, even_ref, odd_ref, cells, far_out, send_out, keep_out, total):
    size_x, size_y, rows3, size_z = act_ref.shape
    channels = rows3 // 3
    ix, iy = lax.axis_index("gx"), lax.axis_index("gy")
    near = jnp.where(ix % 2 == 0, size_x + 1, 0)
    zero = jnp.zeros((channels, size_z), BF16)
    for x in range(size_x + 1):
        at = x + 1 if x < size_x else near
        for y in range(size_y):
            cells[at, y + 1] = grad_ref[x, y] if x < size_x else near_ref[y]
        low = jnp.where(iy % 2 == 0, odd_ref[x], even_ref[x])
        high = jnp.where(iy % 2 == 0, even_ref[x], odd_ref[x])
        cells[at, 0] = jnp.where(iy == 0, zero, low)
        cells[at, size_y + 1] = jnp.where(iy == lax.axis_size("gy") - 1, zero, high)
    for y in range(size_y + 2):
        cells[size_x + 1 - near, y] = zero
    edge = jnp.where(ix % 2 == 0, 0, size_x - 1)
    far_out[: size_y + 2] = cells[edge + 1]
    for y in range(size_y):
        far_out[size_y + 2 + y] = act_ref[edge, y, channels : 2 * channels]
    acc = jnp.zeros((9 * channels, rows3), F32)
    for x in range(size_x):
        for y in range(0, size_y, 2):
            lhs = jnp.concatenate([stacked(cells, x, y), stacked(cells, x, y + 1)], axis=1)
            rhs = jnp.concatenate([act_ref[x, y], act_ref[x, y + 1]], axis=1)
            acc = acc + lax.dot_general(lhs, rhs, (((1,), (1,)), ((), ())), preferred_element_type=F32)
    pack(acc, total)
    split(total, send_out, keep_out)


def across_body(both, act_ref, cells, far_ref, send_out, keep_out, total):
    size_x, size_y, rows3, size_z = act_ref.shape
    channels = rows3 // 3
    ix = lax.axis_index("gx")
    even = ix % 2 == 0
    edge = jnp.where(even, 0, size_x - 1)

    def product(grads, acts):
        acc = jnp.zeros((3 * channels, rows3), F32)
        for y in range(0, size_y, 2):
            lhs = [jnp.concatenate([grads(y + k - b + 2) for b in range(3)], axis=0) for k in range(2)]
            rhs = [acts(y), acts(y + 1)]
            acc = acc + lax.dot_general(
                jnp.concatenate(lhs, axis=1),
                jnp.concatenate(rhs, axis=1),
                (((1,), (1,)), ((), ())),
                preferred_element_type=F32,
            )
        return acc

    def offsets(y):
        act = far_ref[size_y + 2 + y].astype(F32)
        return jnp.concatenate([shift_z(act, 1), act, shift_z(act, -1)], axis=0).astype(BF16)

    own = product(lambda y: far_ref[y], lambda y: act_ref[edge, y])
    other = product(lambda y: cells[edge + 1, y], offsets) if both else jnp.zeros_like(own)
    outside = (ix == 0) | (ix == lax.axis_size("gx") - 1)
    first = jnp.where(outside, 0.0, jnp.where(even, other, own))
    last = jnp.where(outside, 0.0, jnp.where(even, own, other))
    pack(jnp.concatenate([first, jnp.zeros_like(own), last], axis=0), total)
    split(total, send_out, keep_out)


def finish_body(scale, mine_ref, other_ref, out_ref, total):
    channels = out_ref.shape[-1]
    half = mine_ref.shape[0]
    mine = half_of()
    total[pl.ds(pl.multiple_of(mine * half, 8), half)] = mine_ref[...] / scale
    total[pl.ds(pl.multiple_of((1 - mine) * half, 8), half)] = other_ref[...] / scale
    rows = 9 * channels // 4
    for ab in range(9):
        for c in range(3):
            first = ab * channels
            parts = []
            for r in range(first, first + channels, 8):
                if r < 3 * rows:
                    parts.append(total[r : r + 8, c * channels : (c + 1) * channels])
                else:
                    q = c * rows + r - 3 * rows
                    parts.append(total[q : q + 8, 3 * channels : 4 * channels])
            out_ref[ab // 3, ab % 3, c] = jnp.concatenate(parts, axis=0)


def inputs_body(cells_ref, far_ref, kernel_ref, out_ref, cells):
    channels, size_x, size_y, size_z = out_ref.shape
    ix = lax.axis_index("gx")
    cells[...] = cells_ref[...]

    @pl.when((ix != 0) & (ix != lax.axis_size("gx") - 1))
    def _():
        cells[jnp.where(ix % 2 == 0, 0, size_x + 1)] = far_ref[: size_y + 2]

    taps = jnp.concatenate(
        [
            jnp.concatenate([kernel_ref[a, b, c] for a in range(3) for b in range(3)], axis=0).astype(F32)
            for c in range(3)
        ],
        axis=1,
    )
    taps = jnp.transpose(taps).astype(BF16)
    for x in range(size_x):
        rows = []
        for y in range(0, size_y, 2):
            rhs = jnp.concatenate([stacked(cells, x, y), stacked(cells, x, y + 1)], axis=1)
            terms = jnp.dot(taps, rhs, preferred_element_type=F32)
            for k in range(2):
                part = terms[:, k * size_z : (k + 1) * size_z]
                row = shift_z(part[:channels], -1) + part[channels : 2 * channels]
                rows.append(row + shift_z(part[2 * channels :], 1))
        out_ref[:, x] = jnp.swapaxes(jnp.stack(rows), 0, 1).astype(BF16)


def shards(activation, out_grad, kernel):
    channels, size_x, size_y, size_z = activation.shape
    counts = (lax.axis_size("gx"), lax.axis_size("gy"))
    nx, ny = counts
    shape = jax.ShapeDtypeStruct
    volume = channels * size_x * size_y * size_z

    def permute(value, partner):
        return lax.ppermute(value, BOTH, pairs(counts, partner))

    def core(ix, iy):
        return ix ^ 1, iy

    def odd_x(ix, iy):
        return (ix + 1 if ix % 2 else ix - 1) % nx, iy

    def even_y(ix, iy):
        return ix, iy ^ 1

    def odd_y(ix, iy):
        if iy in (0, ny - 1):
            return ix ^ 1, iy
        return ix, (iy + 1 if iy % 2 else iy - 1)

    def call(name, body, out_shape, arrays, scratch=(), flops=0, in_specs=None, limit=16 << 20):
        outs = out_shape if isinstance(out_shape, tuple) else (out_shape,)
        nbytes = sum(a.size * a.dtype.itemsize for a in (*arrays, *outs))
        return pl.pallas_call(
            body,
            out_shape=out_shape,
            in_specs=in_specs or [VMEM] * len(arrays),
            out_specs=jax.tree.map(lambda _: VMEM, out_shape),
            scratch_shapes=list(scratch),
            compiler_params=params(limit),
            cost_estimate=cost(flops, nbytes),
            name=name,
        )(*arrays)

    grad, near = call(
        "gradient",
        gradient_body,
        (shape((size_x, size_y, channels, size_z), BF16), shape((size_y, channels, size_z), BF16)),
        (out_grad,),
        (
            pltpu.VMEM((size_x, channels, size_y, size_z), BF16),
            pltpu.SemaphoreType.DMA((size_x,)),
        ),
        in_specs=[pl.BlockSpec(memory_space=pltpu.HBM)],
        limit=16 << 20,
    )
    near = permute(near, core)
    face = shape((size_x + 1, channels, size_z), BF16)
    even, odd = call("faces", faces_body, (face, face), (grad, near))
    odd = permute(odd, odd_y)
    even = permute(even, even_y)
    act = call(
        "activation",
        activation_body,
        shape((size_x, size_y, 3 * channels, size_z), BF16),
        (activation,),
    )
    rows = (9 * 3 * channels * channels // 128 + 15) // 16 * 8
    half = shape((rows, 128), F32)
    whole = pltpu.VMEM((2 * rows, 128), F32)
    cells, far, send, total = call(
        "weights",
        weights_body,
        (
            shape((size_x + 2, size_y + 2, channels, size_z), BF16),
            shape((2 * size_y + 2, channels, size_z), BF16),
            half,
            half,
        ),
        (act, grad, near, even, odd),
        (whole,),
        flops=54 * channels * volume,
    )
    both = nx == 4
    if both:
        total = total + permute(send, core)
    far = permute(far, odd_x)
    across = functools.partial(across_body, both)
    far_send, far_total = call("across", across, (half, half), (act, cells, far), (whole,), flops=volume)
    if both:
        far_total = far_total + permute(far_send, core)
    else:
        total = total + far_total + permute(send + far_send, core)
    step = 2
    while step < nx:
        total = total + permute(total, lambda ix, iy: (ix ^ 1 ^ step, iy))
        step *= 2
    if both:
        total = total + far_total
    grad_input = call(
        "inputs",
        inputs_body,
        shape(activation.shape, BF16),
        (cells, far, kernel),
        (pltpu.VMEM(cells.shape, BF16),),
        flops=54 * channels * volume,
    )
    step = 1
    while step < ny:
        total = total + permute(total, lambda ix, iy: (ix ^ 1, iy ^ step))
        if step == 1:
            total, grad_input = lax.optimization_barrier((total, grad_input))
        step *= 2
    other = permute(total, core)
    cell_count = nx * size_x * ny * size_y * size_z
    finish = functools.partial(finish_body, float(cell_count) ** 0.5)
    grad_kernel = call("finish", finish, shape(kernel.shape, F32), (total, other), (whole,))
    return (grad_input, grad_kernel)


def solution(mesh):
    return jax.shard_map(
        shards,
        mesh=mesh,
        in_specs=(P(None, "gx", "gy", None), P(None, "gx", "gy", None), P()),
        out_specs=(P(None, "gx", "gy", None), P()),
        check_vma=False,
    )
```

time: 36.1 us -> 33.5 us (0.928)
  waiting for transfers between devices: 22.5 us -> 20.9 us
  local copies, waits for them, and re-layouts: 1.81 us -> 0.91 us
  starting transfers between devices: 7.85 us -> 7.19 us
  Pallas kernels: 3.08 us -> 3.6 us
    ppermute x10 -> x11, waiting for transfers between devices: 22.5 us -> 20.9 us  [permute(): return lax.ppermute(value, BOTH, pairs(counts, partner))]
    unnamed x6, local copies, waits for them, and re-layouts: 1.81 us -> 0.91 us
    ppermute x10 -> x11, starting transfers between devices: 7.85 us -> 7.19 us  [permute(): return lax.ppermute(value, BOTH, pairs(counts, partner))]
    pallas_call x5 -> x7, Pallas kernels: 3.08 us -> 3.6 us  [call(): pl.pallas_call(body, out_shape=out_shape, in_specs=in_specs or [VMEM] * l...]
  transfers between devices with their start and end apart: 10 -> 11, of which waited for: 8 -> 10; matrix products, arithmetic and copies ran while one was open for 0% -> 0% of each run, Pallas kernels for 4% -> 6%
where the time goes in v2:
time: 33.5 us; the launch traced here: 33.3 us
  waiting for transfers between devices  20.9 us (62%)
  starting transfers between devices  7.19 us (21%)
  Pallas kernels  3.6 us (11%)
  local copies, waits for them, and re-layouts  0.91 us (3%)
  between operations  0.71 us (2%)
    ppermute x11, waiting for transfers between devices, permute(): return lax.ppermute(value, BOTH, pairs(counts, partner))  20.9 us
    ppermute x11, starting transfers between devices, permute(): return lax.ppermute(value, BOTH, pairs(counts, partner))  7.19 us
    pallas_call x7, Pallas kernels, call(): pl.pallas_call(body, out_shape=out_shape, in_specs=in_specs or [VMEM] * l...  3.6 us
    unnamed x6, local copies, waits for them, and re-layouts  0.91 us
  transfers between devices with their start and end apart: 11, of which 10 were waited for; matrix products, arithmetic and copies ran while one was open for 0% of the time, Pallas kernels for 6%

profile of v2, /device:TPU:25, one launch (start us, length us, event | category | flops | bytes accessed | tf_op | source)
XLA Modules:
  0.0 33.3 jit_solution(3130918938465107428)
XLA Ops:
  0.6 0.9 %copy-done.1 = bf16[32,4,4,128]{3,2,1,0:T(4,128)(2,1)S(1)} copy-done((bf16[32,4,4,128]{3,2,1,0:T(4,128)(2,1)S(1)}, bf16[32,4,4,128]{3,2,1,0:T(4,128)(2,1)}, u32[]{:S(2)}) %copy-start.1) | copy-done | bytes 131096
  1.5 0.2 gradient.1
  1.7 0.7 %collective-permute-start = (bf16[4,32,128]{2,1,0:T(8,128)(2,1)S(1)}, bf16[4,32,128]{2,1,0:T(8,128)(2,1)S(1)}, u32[]{:S(2)}, u32[]{:S(2)}) collective-permute-start(bf16[4,32,128]{2,1,0:T(8,128)(2,1)S(1)} %get-tuple-element.15), channel_id=1, source_target_pairs={{0,8},{1,9},{2,10},{3,11},{4,12},{5,13},{6,14},{7,15},{8,0},{9,1},... | collective-permute-start | bytes 98312 | tf_op jit(solution)/shard_map/ppermute | solution.py:217
  2.5 0.9 %collective-permute-done.near_ref = bf16[4,32,128]{2,1,0:T(8,128)(2,1)S(1)} collective-permute-done((bf16[4,32,128]{2,1,0:T(8,128)(2,1)S(1)}, bf16[4,32,128]{2,1,0:T(8,128)(2,1)S(1)}, u32[]{:S(2)}, u32[]{:S(2)}) %collective-permute-start) | collective-permute-done | bytes 32800 | tf_op jit(solution)/shard_map/ppermute | solution.py:217
  3.3 1.2 %collective-permute-start.1 = (bf16[5,32,128]{2,1,0:T(8,128)(2,1)S(1)}, bf16[5,32,128]{2,1,0:T(8,128)(2,1)S(1)}, u32[]{:S(2)}, u32[]{:S(2)}) collective-permute-start(bf16[5,32,128]{2,1,0:T(8,128)(2,1)S(1)} %get-tuple-element.16), channel_id=1, source_target_pairs={{0,1},{1,0},{2,3},{3,2},{4,5},{5,4},{6,7},{7,6},{8,9},{9,8},{10,11... | collective-permute-start | bytes 122888 | tf_op jit(solution)/shard_map/ppermute | solution.py:217
  4.8 1.3 %collective-permute-done.1.even_ref = bf16[5,32,128]{2,1,0:T(8,128)(2,1)S(1)} collective-permute-done((bf16[5,32,128]{2,1,0:T(8,128)(2,1)S(1)}, bf16[5,32,128]{2,1,0:T(8,128)(2,1)S(1)}, u32[]{:S(2)}, u32[]{:S(2)}) %collective-permute-start.1) | collective-permute-done | bytes 40992 | tf_op jit(solution)/shard_map/ppermute | solution.py:217
  6.2 2.1 %collective-permute-done.2.odd_ref = bf16[5,32,128]{2,1,0:T(8,128)(2,1)S(1)} collective-permute-done((bf16[5,32,128]{2,1,0:T(8,128)(2,1)S(1)}, bf16[5,32,128]{2,1,0:T(8,128)(2,1)S(1)}, u32[]{:S(2)}, u32[]{:S(2)}) %collective-permute-start.2) | collective-permute-done | bytes 40992 | tf_op jit(solution)/shard_map/ppermute | solution.py:217
  8.3 0.6 %weights.1 = (bf16[6,6,32,128]{3,2,1,0:T(8,128)(2,1)S(1)}, bf16[10,32,128]{2,1,0:T(8,128)(2,1)S(1)}, f32[112,128]{1,0:T(8,128)S(1)}, f32[112,128]{1,0:T(8,128)S(1)}) custom-call(bf16[4,4,96,128]{3,2,1,0:T(8,128)(2,1)S(1)} %activation.1.act_ref, bf16[4,4,32,128]{3,2,1,0:T(8,128)(2,1)S(1)} %get-tuple-element.14.grad_ref, ...), custom_call_target="tpu_custom_call" | custom-call | flops 113246208 | bytes 1130496 | tf_op jit(solution)/shard_map/weights/pallas_call | solution.py:236
  8.9 2.9 %collective-permute-start.5 = (bf16[10,32,128]{2,1,0:T(8,128)(2,1)S(1)}, bf16[10,32,128]{2,1,0:T(8,128)(2,1)S(1)}, u32[]{:S(2)}, u32[]{:S(2)}) collective-permute-start(bf16[10,32,128]{2,1,0:T(8,128)(2,1)S(1)} %get-tuple-element.21), channel_id=1, source_target_pairs={{0,24},{1,25},{2,26},{3,27},{4,28},{5,29},{6,30},{7,31},{8,16},{9,... | collective-permute-start | bytes 245768 | tf_op jit(solution)/shard_map/ppermute | solution.py:217
  11.9 1.2 %collective-permute-done.3 = f32[112,128]{1,0:T(8,128)S(1)} collective-permute-done((f32[112,128]{1,0:T(8,128)S(1)}, f32[112,128]{1,0:T(8,128)S(1)}, u32[]{:S(2)}, u32[]{:S(2)}) %collective-permute-start.3) | collective-permute-done | bytes 57376 | tf_op jit(solution)/shard_map/ppermute | solution.py:217
  13.1 0.3 collective-permute-start.4
  13.5 1.6 %collective-permute-done.5.far_ref = bf16[10,32,128]{2,1,0:T(8,128)(2,1)S(1)} collective-permute-done((bf16[10,32,128]{2,1,0:T(8,128)(2,1)S(1)}, bf16[10,32,128]{2,1,0:T(8,128)(2,1)S(1)}, u32[]{:S(2)}, u32[]{:S(2)}) %collective-permute-start.5) | collective-permute-done | bytes 81952 | tf_op jit(solution)/shard_map/ppermute | solution.py:217
  15.1 0.4 %across.1 = (f32[112,128]{1,0:T(8,128)S(1)}, f32[112,128]{1,0:T(8,128)S(1)}) custom-call(bf16[4,4,96,128]{3,2,1,0:T(8,128)(2,1)S(1)} %activation.1.act_ref, bf16[6,6,32,128]{3,2,1,0:T(8,128)(2,1)S(1)} %get-tuple-element.20.cells.cells_ref, bf16[10,32,128]{2,1,0:T(8,128)(2,1)S(1)} %collective-permute-done.5.far_ref), custom_call_target="tpu_custom_call" | custom-call | flops 65536 | bytes 884736 | tf_op jit(solution)/shard_map/across/pallas_call | solution.py:236
  15.5 0.5 %collective-permute-start.6 = (f32[112,128]{1,0:T(8,128)S(1)}, f32[112,128]{1,0:T(8,128)S(1)}, u32[]{:S(2)}, u32[]{:S(2)}) collective-permute-start(f32[112,128]{1,0:T(8,128)S(1)} %get-tuple-element.23), channel_id=1, source_target_pairs={{0,8},{1,9},{2,10},{3,11},{4,12},{5,13},{6,14},{7,15},{8,0},{9,1},... | collective-permute-start | bytes 172040 | tf_op jit(solution)/shard_map/ppermute | solution.py:217
  16.0 0.9 %collective-permute-done.4 = f32[112,128]{1,0:T(8,128)S(1)} collective-permute-done((f32[112,128]{1,0:T(8,128)S(1)}, f32[112,128]{1,0:T(8,128)S(1)}, u32[]{:S(2)}, u32[]{:S(2)}) %collective-permute-start.4) | collective-permute-done | bytes 57376 | tf_op jit(solution)/shard_map/ppermute | solution.py:217
  17.0 1.3 %inputs.1 = bf16[32,4,4,128]{3,2,1,0:T(4,128)(2,1)} custom-call(bf16[6,6,32,128]{3,2,1,0:T(8,128)(2,1)S(1)} %get-tuple-element.20.cells.cells_ref, bf16[10,32,128]{2,1,0:T(8,128)(2,1)S(1)} %collective-permute-done.5.far_ref, bf16[3,3,3,32,32]{4,3,2,1,0:T(8,128)(2,1)S(1)} %copy-done), custom_call_target="tpu_custom_call" | custom-call | flops 113246208 | bytes 563200 | tf_op jit(solution)/shard_map/inputs/pallas_call | solution.py:236
  18.3 2.5 %collective-permute-done.7 = f32[112,128]{1,0:T(8,128)S(1)} collective-permute-done((f32[112,128]{1,0:T(8,128)S(1)}, f32[112,128]{1,0:T(8,128)S(1)}, u32[]{:S(2)}, u32[]{:S(2)}) %collective-permute-start.7) | collective-permute-done | bytes 57376 | tf_op jit(solution)/shard_map/ppermute | solution.py:217
  20.8 0.5 %collective-permute-start.8 = (f32[112,128]{1,0:T(8,128)S(1)}, f32[112,128]{1,0:T(8,128)S(1)}, u32[]{:S(2)}, u32[]{:S(2)}) collective-permute-start(f32[112,128]{1,0:T(8,128)S(1)} %add.25), channel_id=1, source_target_pairs={{0,10},{1,11},{2,8},{3,9},{4,14},{5,15},{6,12},{7,13},{8,2},{9,3},... | collective-permute-start | bytes 172040 | tf_op jit(solution)/shard_map/ppermute | solution.py:217
  21.3 3.5 %collective-permute-done.8 = f32[112,128]{1,0:T(8,128)S(1)} collective-permute-done((f32[112,128]{1,0:T(8,128)S(1)}, f32[112,128]{1,0:T(8,128)S(1)}, u32[]{:S(2)}, u32[]{:S(2)}) %collective-permute-start.8) | collective-permute-done | bytes 57376 | tf_op jit(solution)/shard_map/ppermute | solution.py:217
  24.8 0.4 %collective-permute-start.9 = (f32[112,128]{1,0:T(8,128)S(1)}, f32[112,128]{1,0:T(8,128)S(1)}, u32[]{:S(2)}, u32[]{:S(2)}) collective-permute-start(f32[112,128]{1,0:T(8,128)S(1)} %add.26), channel_id=1, source_target_pairs={{0,12},{1,13},{2,14},{3,15},{4,8},{5,9},{6,10},{7,11},{8,4},{9,5},... | collective-permute-start | bytes 172040 | tf_op jit(solution)/shard_map/ppermute | solution.py:217
  25.2 5.9 %collective-permute-done.9 = f32[112,128]{1,0:T(8,128)S(1)} collective-permute-done((f32[112,128]{1,0:T(8,128)S(1)}, f32[112,128]{1,0:T(8,128)S(1)}, u32[]{:S(2)}, u32[]{:S(2)}) %collective-permute-start.9) | collective-permute-done | bytes 57376 | tf_op jit(solution)/shard_map/ppermute | solution.py:217
  31.0 0.5 %collective-permute-start.10 = (f32[112,128]{1,0:T(8,128)S(1)}, f32[112,128]{1,0:T(8,128)S(1)}, u32[]{:S(2)}, u32[]{:S(2)}) collective-permute-start(f32[112,128]{1,0:T(8,128)S(1)} %add.27.mine_ref), channel_id=1, source_target_pairs={{0,8},{1,9},{2,10},{3,11},{4,12},{5,13},{6,14},{7,15},{8,0},{9,1},... | collective-permute-start | bytes 172040 | tf_op jit(solution)/shard_map/ppermute | solution.py:217
  31.5 0.9 %collective-permute-done.10.other_ref = f32[112,128]{1,0:T(8,128)S(1)} collective-permute-done((f32[112,128]{1,0:T(8,128)S(1)}, f32[112,128]{1,0:T(8,128)S(1)}, u32[]{:S(2)}, u32[]{:S(2)}) %collective-permute-start.10) | collective-permute-done | bytes 57376 | tf_op jit(solution)/shard_map/ppermute | solution.py:217
  32.4 0.9 %finish.1 = f32[3,3,3,32,32]{4,3,2,1,0:T(8,128)} custom-call(f32[112,128]{1,0:T(8,128)S(1)} %add.27.mine_ref, f32[112,128]{1,0:T(8,128)S(1)} %collective-permute-done.10.other_ref), custom_call_target="tpu_custom_call" | custom-call | bytes 225280 | tf_op jit(solution)/shard_map/finish/pallas_call | solution.py:236
  (16 shorter events, 0.4 us)
Async XLA Ops:
  0.6 0.9 %copy-start.1 = (bf16[32,4,4,128]{3,2,1,0:T(4,128)(2,1)S(1)}, bf16[32,4,4,128]{3,2,1,0:T(4,128)(2,1)}, u32[]{:S(2)}) copy-start(bf16[32,4,4,128]{3,2,1,0:T(4,128)(2,1)} %grad_hbm.1) | copy-start | bytes 393220
  1.5 3.1 %copy-start.2 = (bf16[32,4,4,128]{3,2,1,0:T(4,128)(2,1)S(1)}, bf16[32,4,4,128]{3,2,1,0:T(4,128)(2,1)}, u32[]{:S(2)}) copy-start(bf16[32,4,4,128]{3,2,1,0:T(4,128)(2,1)} %act_ref.1) | copy-start | bytes 393220
  1.7 1.6 %collective-permute-start = (bf16[4,32,128]{2,1,0:T(8,128)(2,1)S(1)}, bf16[4,32,128]{2,1,0:T(8,128)(2,1)S(1)}, u32[]{:S(2)}, u32[]{:S(2)}) collective-permute-start(bf16[4,32,128]{2,1,0:T(8,128)(2,1)S(1)} %get-tuple-element.15), channel_id=1, source_target_pairs={{0,8},{1,9},{2,10},{3,11},{4,12},{5,13},{6,14},{7,15},{8,0},{9,1},... | collective-permute-start | bytes 98312 | tf_op jit(solution)/shard_map/ppermute | solution.py:217
  3.3 2.9 %collective-permute-start.1 = (bf16[5,32,128]{2,1,0:T(8,128)(2,1)S(1)}, bf16[5,32,128]{2,1,0:T(8,128)(2,1)S(1)}, u32[]{:S(2)}, u32[]{:S(2)}) collective-permute-start(bf16[5,32,128]{2,1,0:T(8,128)(2,1)S(1)} %get-tuple-element.16), channel_id=1, source_target_pairs={{0,1},{1,0},{2,3},{3,2},{4,5},{5,4},{6,7},{7,6},{8,9},{9,8},{10,11... | collective-permute-start | bytes 122888 | tf_op jit(solution)/shard_map/ppermute | solution.py:217
  4.6 3.8 %collective-permute-start.2 = (bf16[5,32,128]{2,1,0:T(8,128)(2,1)S(1)}, bf16[5,32,128]{2,1,0:T(8,128)(2,1)S(1)}, u32[]{:S(2)}, u32[]{:S(2)}) collective-permute-start(bf16[5,32,128]{2,1,0:T(8,128)(2,1)S(1)} %get-tuple-element.17), channel_id=1, source_target_pairs={{0,8},{1,2},{2,1},{3,4},{4,3},{5,6},{6,5},{7,15},{8,0},{9,10},{10,... | collective-permute-start | bytes 122888 | tf_op jit(solution)/shard_map/ppermute | solution.py:217
  8.9 6.1 %collective-permute-start.5 = (bf16[10,32,128]{2,1,0:T(8,128)(2,1)S(1)}, bf16[10,32,128]{2,1,0:T(8,128)(2,1)S(1)}, u32[]{:S(2)}, u32[]{:S(2)}) collective-permute-start(bf16[10,32,128]{2,1,0:T(8,128)(2,1)S(1)} %get-tuple-element.21), channel_id=1, source_target_pairs={{0,24},{1,25},{2,26},{3,27},{4,28},{5,29},{6,30},{7,31},{8,16},{9,... | collective-permute-start | bytes 245768 | tf_op jit(solution)/shard_map/ppermute | solution.py:217
  11.9 1.2 %collective-permute-start.3 = (f32[112,128]{1,0:T(8,128)S(1)}, f32[112,128]{1,0:T(8,128)S(1)}, u32[]{:S(2)}, u32[]{:S(2)}) collective-permute-start(f32[112,128]{1,0:T(8,128)S(1)} %get-tuple-element.19), channel_id=1, source_target_pairs={{0,8},{1,9},{2,10},{3,11},{4,12},{5,13},{6,14},{7,15},{8,0},{9,1},... | collective-permute-start | bytes 172040 | tf_op jit(solution)/shard_map/ppermute | solution.py:217
  13.1 3.7 %collective-permute-start.4 = (f32[112,128]{1,0:T(8,128)S(1)}, f32[112,128]{1,0:T(8,128)S(1)}, u32[]{:S(2)}, u32[]{:S(2)}) collective-permute-start(f32[112,128]{1,0:T(8,128)S(1)} %add.21), channel_id=1, source_target_pairs={{0,24},{1,25},{2,26},{3,27},{4,28},{5,29},{6,30},{7,31},{8,16},{9,... | collective-permute-start | bytes 172040 | tf_op jit(solution)/shard_map/ppermute | solution.py:217
  15.5 1.5 %copy-start = (bf16[3,3,3,32,32]{4,3,2,1,0:T(8,128)(2,1)S(1)}, bf16[3,3,3,32,32]{4,3,2,1,0:T(8,128)(2,1)}, u32[]{:S(2)}) copy-start(bf16[3,3,3,32,32]{4,3,2,1,0:T(8,128)(2,1)} %kernel_ref.1) | copy-start | bytes 165892
  15.5 1.4 %collective-permute-start.6 = (f32[112,128]{1,0:T(8,128)S(1)}, f32[112,128]{1,0:T(8,128)S(1)}, u32[]{:S(2)}, u32[]{:S(2)}) collective-permute-start(f32[112,128]{1,0:T(8,128)S(1)} %get-tuple-element.23), channel_id=1, source_target_pairs={{0,8},{1,9},{2,10},{3,11},{4,12},{5,13},{6,14},{7,15},{8,0},{9,1},... | collective-permute-start | bytes 172040 | tf_op jit(solution)/shard_map/ppermute | solution.py:217
  16.9 3.9 %collective-permute-start.7 = (f32[112,128]{1,0:T(8,128)S(1)}, f32[112,128]{1,0:T(8,128)S(1)}, u32[]{:S(2)}, u32[]{:S(2)}) collective-permute-start(f32[112,128]{1,0:T(8,128)S(1)} %add_add_fusion), channel_id=1, source_target_pairs={{0,9},{1,8},{2,11},{3,10},{4,13},{5,12},{6,15},{7,14},{8,1},{9,0},... | collective-permute-start | bytes 172040 | tf_op jit(solution)/shard_map/ppermute | solution.py:217
  20.8 3.9 %collective-permute-start.8 = (f32[112,128]{1,0:T(8,128)S(1)}, f32[112,128]{1,0:T(8,128)S(1)}, u32[]{:S(2)}, u32[]{:S(2)}) collective-permute-start(f32[112,128]{1,0:T(8,128)S(1)} %add.25), channel_id=1, source_target_pairs={{0,10},{1,11},{2,8},{3,9},{4,14},{5,15},{6,12},{7,13},{8,2},{9,3},... | collective-permute-start | bytes 172040 | tf_op jit(solution)/shard_map/ppermute | solution.py:217
  24.8 6.2 %collective-permute-start.9 = (f32[112,128]{1,0:T(8,128)S(1)}, f32[112,128]{1,0:T(8,128)S(1)}, u32[]{:S(2)}, u32[]{:S(2)}) collective-permute-start(f32[112,128]{1,0:T(8,128)S(1)} %add.26), channel_id=1, source_target_pairs={{0,12},{1,13},{2,14},{3,15},{4,8},{5,9},{6,10},{7,11},{8,4},{9,5},... | collective-permute-start | bytes 172040 | tf_op jit(solution)/shard_map/ppermute | solution.py:217
  31.0 1.4 %collective-permute-start.10 = (f32[112,128]{1,0:T(8,128)S(1)}, f32[112,128]{1,0:T(8,128)S(1)}, u32[]{:S(2)}, u32[]{:S(2)}) collective-permute-start(f32[112,128]{1,0:T(8,128)S(1)} %add.27.mine_ref), channel_id=1, source_target_pairs={{0,8},{1,9},{2,10},{3,11},{4,12},{5,13},{6,14},{7,15},{8,0},{9,1},... | collective-permute-start | bytes 172040 | tf_op jit(solution)/shard_map/ppermute | solution.py:217

commit v3 on v2

--- a/solution.py
+++ b/solution.py
@@ -79,52 +79,87 @@
     return jnp.concatenate([cells[x - a + 2, y - b + 2] for a in range(3) for b in range(3)], axis=0)
 
 
-def pack(terms, total):
+def pack_half(terms, half, out):
     channels = terms.shape[1] // 3
-    rows = 9 * channels // 4
-    spread = [terms[3 * rows :, k * channels : (k + 1) * channels] for k in range(3)]
-    total[: 3 * rows] = jnp.concatenate([terms[: 3 * rows], jnp.concatenate(spread, axis=0)], axis=1)
-    total[3 * rows :] = jnp.zeros((total.shape[0] - 3 * rows, total.shape[1]), F32)
-
-
-def split(total, send_out, keep_out):
-    half = keep_out.shape[0]
+    part = channels // 2
+    count = out.shape[0] // part
+
+    def rows(slot):
+        return pl.ds(pl.multiple_of(slot * channels + half * part, 8), part)
+
+    for k in range(count):
+        main = terms[rows(k)]
+        slot, c = divmod(k, 3)
+        if count + slot < 9:
+            side = terms[rows(count + slot)][:, c * channels : (c + 1) * channels]
+        else:
+            side = jnp.zeros((part, channels), F32)
+        out[k * part : (k + 1) * part] = jnp.concatenate([main, side], axis=1)
+
+
+def split(terms, send_out, keep_out):
     mine = half_of()
-    keep_out[...] = total[pl.ds(pl.multiple_of(mine * half, 8), half)]
-    send_out[...] = total[pl.ds(pl.multiple_of((1 - mine) * half, 8), half)]
-
-
-def weights_body(act_ref, grad_ref, near_ref, even_ref, odd_ref, cells, far_out, send_out, keep_out, total):
+    pack_half(terms, mine, keep_out)
+    pack_half(terms, 1 - mine, send_out)
+
+
+def outer(lhs, rhs):
+    dims = (((1,), (1,)), ((), ()))
+    total = None
+    for k in range(0, len(lhs), 2):
+        term = lax.dot_general(
+            jnp.concatenate(lhs[k : k + 2], axis=1),
+            jnp.concatenate(rhs[k : k + 2], axis=1),
+            dims,
+            preferred_element_type=F32,
+        )
+        total = term if total is None else total + term
+    return total
+
+
+def inner_body(act_ref, grad_ref, near_ref, cells, acc_out):
+    size_x, size_y, rows3, size_z = act_ref.shape
+    even = lax.axis_index("gx") % 2 == 0
+    near = jnp.where(even, size_x + 1, 0)
+    zero = jnp.zeros((rows3 // 3, size_z), BF16)
+    for y in range(size_y + 2):
+        inside = 0 < y <= size_y
+        cells[near, y] = near_ref[y - 1] if inside else zero
+        cells[size_x + 1 - near, y] = zero
+        for x in range(size_x):
+            cells[x + 1, y] = grad_ref[x, y - 1] if inside else zero
+    order = [(x, y) for x in range(size_x) for y in range(size_y)]
+    acc_out[...] = outer([stacked(cells, x, y) for x, y in order], [act_ref[x, y] for x, y in order])
+
+
+def edges_body(act_ref, inner_ref, acc_ref, even_ref, odd_ref, cells, far_out, send_out, keep_out, acc):
     size_x, size_y, rows3, size_z = act_ref.shape
     channels = rows3 // 3
     ix, iy = lax.axis_index("gx"), lax.axis_index("gy")
     near = jnp.where(ix % 2 == 0, size_x + 1, 0)
     zero = jnp.zeros((channels, size_z), BF16)
+    cells[...] = inner_ref[...]
     for x in range(size_x + 1):
         at = x + 1 if x < size_x else near
-        for y in range(size_y):
-            cells[at, y + 1] = grad_ref[x, y] if x < size_x else near_ref[y]
         low = jnp.where(iy % 2 == 0, odd_ref[x], even_ref[x])
         high = jnp.where(iy % 2 == 0, even_ref[x], odd_ref[x])
         cells[at, 0] = jnp.where(iy == 0, zero, low)
         cells[at, size_y + 1] = jnp.where(iy == lax.axis_size("gy") - 1, zero, high)
-    for y in range(size_y + 2):
-        cells[size_x + 1 - near, y] = zero
     edge = jnp.where(ix % 2 == 0, 0, size_x - 1)
     far_out[: size_y + 2] = cells[edge + 1]
     for y in range(size_y):
         far_out[size_y + 2 + y] = act_ref[edge, y, channels : 2 * channels]
-    acc = jnp.zeros((9 * channels, rows3), F32)
-    for x in range(size_x):
-        for y in range(0, size_y, 2):
-            lhs = jnp.concatenate([stacked(cells, x, y), stacked(cells, x, y + 1)], axis=1)
-            rhs = jnp.concatenate([act_ref[x, y], act_ref[x, y + 1]], axis=1)
-            acc = acc + lax.dot_general(lhs, rhs, (((1,), (1,)), ((), ())), preferred_element_type=F32)
-    pack(acc, total)
-    split(total, send_out, keep_out)
-
-
-def across_body(both, act_ref, cells, far_ref, send_out, keep_out, total):
+    acc[...] = acc_ref[...]
+    for b, row, y in ((2, 0, 0), (0, size_y + 1, size_y - 1)):
+        lhs = [jnp.concatenate([cells[x - a + 2, row] for a in range(3)], axis=0) for x in range(size_x)]
+        terms = outer(lhs, [act_ref[x, y] for x in range(size_x)])
+        for a in range(3):
+            first = (3 * a + b) * channels
+            acc[first : first + channels] += terms[a * channels : (a + 1) * channels]
+    split(acc, send_out, keep_out)
+
+
+def across_body(both, act_ref, cells, far_ref, send_out, keep_out, acc):
     size_x, size_y, rows3, size_z = act_ref.shape
     channels = rows3 // 3
     ix = lax.axis_index("gx")
@@ -132,17 +167,8 @@
     edge = jnp.where(even, 0, size_x - 1)
 
     def product(grads, acts):
-        acc = jnp.zeros((3 * channels, rows3), F32)
-        for y in range(0, size_y, 2):
-            lhs = [jnp.concatenate([grads(y + k - b + 2) for b in range(3)], axis=0) for k in range(2)]
-            rhs = [acts(y), acts(y + 1)]
-            acc = acc + lax.dot_general(
-                jnp.concatenate(lhs, axis=1),
-                jnp.concatenate(rhs, axis=1),
-                (((1,), (1,)), ((), ())),
-                preferred_element_type=F32,
-            )
-        return acc
+        lhs = [jnp.concatenate([grads(y - b + 2) for b in range(3)], axis=0) for y in range(size_y)]
+        return outer(lhs, [acts(y) for y in range(size_y)])
 
     def offsets(y):
         act = far_ref[size_y + 2 + y].astype(F32)
@@ -151,30 +177,24 @@
     own = product(lambda y: far_ref[y], lambda y: act_ref[edge, y])
     other = product(lambda y: cells[edge + 1, y], offsets) if both else jnp.zeros_like(own)
     outside = (ix == 0) | (ix == lax.axis_size("gx") - 1)
-    first = jnp.where(outside, 0.0, jnp.where(even, other, own))
-    last = jnp.where(outside, 0.0, jnp.where(even, own, other))
-    pack(jnp.concatenate([first, jnp.zeros_like(own), last], axis=0), total)
-    split(total, send_out, keep_out)
-
-
-def finish_body(scale, mine_ref, other_ref, out_ref, total):
-    channels = out_ref.shape[-1]
-    half = mine_ref.shape[0]
-    mine = half_of()
-    total[pl.ds(pl.multiple_of(mine * half, 8), half)] = mine_ref[...] / scale
-    total[pl.ds(pl.multiple_of((1 - mine) * half, 8), half)] = other_ref[...] / scale
-    rows = 9 * channels // 4
-    for ab in range(9):
+    rows = 3 * channels
+    acc[:rows] = jnp.where(outside, 0.0, jnp.where(even, other, own))
+    acc[rows : 2 * rows] = jnp.zeros_like(own)
+    acc[2 * rows :] = jnp.where(outside, 0.0, jnp.where(even, own, other))
+    split(acc, send_out, keep_out)
+
+
+def finish_body(scale, half_ref, *refs):
+    out_ref = refs[-1]
+    part, channels = out_ref.shape[-2:]
+    count = half_ref.shape[0] // part
+    for k in range(count):
+        rows = half_ref[k * part : (k + 1) * part] / scale
         for c in range(3):
-            first = ab * channels
-            parts = []
-            for r in range(first, first + channels, 8):
-                if r < 3 * rows:
-                    parts.append(total[r : r + 8, c * channels : (c + 1) * channels])
-                else:
-                    q = c * rows + r - 3 * rows
-                    parts.append(total[q : q + 8, 3 * channels : 4 * channels])
-            out_ref[ab // 3, ab % 3, c] = jnp.concatenate(parts, axis=0)
+            out_ref[k // 3, k % 3, c] = rows[:, c * channels : (c + 1) * channels]
+        slot, c = divmod(k, 3)
+        if count + slot < 9:
+            out_ref[(count + slot) // 3, (count + slot) % 3, c] = rows[:, 3 * channels :]
 
 
 def inputs_body(cells_ref, far_ref, kernel_ref, out_ref, cells):
@@ -267,28 +287,31 @@
         shape((size_x, size_y, 3 * channels, size_z), BF16),
         (activation,),
     )
-    rows = (9 * 3 * channels * channels // 128 + 15) // 16 * 8
-    half = shape((rows, 128), F32)
-    whole = pltpu.VMEM((2 * rows, 128), F32)
+    cells_shape = shape((size_x + 2, size_y + 2, channels, size_z), BF16)
+    terms = shape((9 * channels, 3 * channels), F32)
+    half = shape((7 * channels // 2, 4 * channels), F32)
+    acc = pltpu.VMEM(terms.shape, F32)
+    cells, inner = call(
+        "inner",
+        inner_body,
+        (cells_shape, terms),
+        (act, grad, near),
+        flops=54 * channels * volume,
+    )
     cells, far, send, total = call(
-        "weights",
-        weights_body,
-        (
-            shape((size_x + 2, size_y + 2, channels, size_z), BF16),
-            shape((2 * size_y + 2, channels, size_z), BF16),
-            half,
-            half,
-        ),
-        (act, grad, near, even, odd),
-        (whole,),
-        flops=54 * channels * volume,
+        "edges",
+        edges_body,
+        (cells_shape, shape((2 * size_y + 2, channels, size_z), BF16), half, half),
+        (act, cells, inner, even, odd),
+        (acc,),
+        flops=12 * channels * volume,
     )
     both = nx == 4
     if both:
         total = total + permute(send, core)
     far = permute(far, odd_x)
     across = functools.partial(across_body, both)
-    far_send, far_total = call("across", across, (half, half), (act, cells, far), (whole,), flops=volume)
+    far_send, far_total = call("across", across, (half, half), (act, cells, far), (acc,), flops=volume)
     if both:
         far_total = far_total + permute(far_send, core)
     else:
@@ -316,7 +339,24 @@
     other = permute(total, core)
     cell_count = nx * size_x * ny * size_y * size_z
     finish = functools.partial(finish_body, float(cell_count) ** 0.5)
-    grad_kernel = call("finish", finish, shape(kernel.shape, F32), (total, other), (whole,))
+
+    def finished(value, mine, *before):
+        return pl.pallas_call(
+            finish,
+            out_shape=shape(kernel.shape, F32),
+            grid=(1,),
+            in_specs=[VMEM] + [pl.BlockSpec(memory_space=pl.ANY)] * len(before),
+            out_specs=pl.BlockSpec(
+                (3, 3, 3, channels // 2, channels),
+                lambda i: (0, 0, 0, half_of() if mine else 1 - half_of(), 0),
+            ),
+            input_output_aliases={1: 0} if before else {},
+            compiler_params=params(),
+            cost_estimate=cost(0, 8 * value.size),
+            name="finish",
+        )(value, *before)
+
+    grad_kernel = finished(other, False, finished(total, True))
     return (grad_input, grad_kernel)
 
 

time: 33.5 us -> 32.9 us (0.982)
  waiting for transfers between devices: 20.9 us -> 19.6 us
  Pallas kernels: 3.6 us -> 4.37 us
    pallas_call x0 -> x2, Pallas kernels: none -> 1.59 us  [finished(): pl.pallas_call(finish, out_shape=shape(kernel.shape, F32), grid=(1,), in_...]
    ppermute x11, waiting for transfers between devices: 20.9 us -> 19.6 us  [permute(): return lax.ppermute(value, BOTH, pairs(counts, partner))]
    pallas_call x7, Pallas kernels: 3.6 us -> 2.77 us  [call(): pl.pallas_call(body, out_shape=out_shape, in_specs=in_specs or [VMEM] * l...]
  transfers between devices with their start and end apart: 11 -> 11, of which waited for: 10 -> 10; matrix products, arithmetic and copies ran while one was open for 0% -> 0% of each run, Pallas kernels for 6% -> 9%
where the time goes in v3:
time: 32.9 us; the launch traced here: 32.8 us
  waiting for transfers between devices  19.6 us (60%)
  starting transfers between devices  7.11 us (22%)
  Pallas kernels  4.37 us (13%)
  local copies, waits for them, and re-layouts  0.91 us (3%)
  between operations  0.73 us (2%)
    ppermute x11, waiting for transfers between devices, permute(): return lax.ppermute(value, BOTH, pairs(counts, partner))  19.6 us
    ppermute x11, starting transfers between devices, permute(): return lax.ppermute(value, BOTH, pairs(counts, partner))  7.11 us
    pallas_call x7, Pallas kernels, call(): pl.pallas_call(body, out_shape=out_shape, in_specs=in_specs or [VMEM] * l...  2.77 us
    pallas_call x2, Pallas kernels, finished(): pl.pallas_call(finish, out_shape=shape(kernel.shape, F32), grid=(1,), in_...  1.59 us
    unnamed x6, local copies, waits for them, and re-layouts  0.91 us
  transfers between devices with their start and end apart: 11, of which 10 were waited for; matrix products, arithmetic and copies ran while one was open for 0% of the time, Pallas kernels for 9%

profile of v3, /device:TPU:25, one launch (start us, length us, event | category | flops | bytes accessed | tf_op | source)
XLA Modules:
  0.0 32.8 jit_solution(5142035352907747576)
XLA Ops:
  0.6 0.9 %copy-done.1 = bf16[32,4,4,128]{3,2,1,0:T(4,128)(2,1)S(1)} copy-done((bf16[32,4,4,128]{3,2,1,0:T(4,128)(2,1)S(1)}, bf16[32,4,4,128]{3,2,1,0:T(4,128)(2,1)}, u32[]{:S(2)}) %copy-start.1) | copy-done | bytes 131096
  1.7 0.7 %collective-permute-start = (bf16[4,32,128]{2,1,0:T(8,128)(2,1)S(1)}, bf16[4,32,128]{2,1,0:T(8,128)(2,1)S(1)}, u32[]{:S(2)}, u32[]{:S(2)}) collective-permute-start(bf16[4,32,128]{2,1,0:T(8,128)(2,1)S(1)} %get-tuple-element.17), channel_id=1, source_target_pairs={{0,8},{1,9},{2,10},{3,11},{4,12},{5,13},{6,14},{7,15},{8,0},{9,1},... | collective-permute-start | bytes 98312 | tf_op jit(solution)/shard_map/ppermute | solution.py:237
  2.5 0.9 %collective-permute-done.near_ref = bf16[4,32,128]{2,1,0:T(8,128)(2,1)S(1)} collective-permute-done((bf16[4,32,128]{2,1,0:T(8,128)(2,1)S(1)}, bf16[4,32,128]{2,1,0:T(8,128)(2,1)S(1)}, u32[]{:S(2)}, u32[]{:S(2)}) %collective-permute-start) | collective-permute-done | bytes 32800 | tf_op jit(solution)/shard_map/ppermute | solution.py:237
  3.3 1.2 %collective-permute-start.1 = (bf16[5,32,128]{2,1,0:T(8,128)(2,1)S(1)}, bf16[5,32,128]{2,1,0:T(8,128)(2,1)S(1)}, u32[]{:S(2)}, u32[]{:S(2)}) collective-permute-start(bf16[5,32,128]{2,1,0:T(8,128)(2,1)S(1)} %get-tuple-element.20), channel_id=1, source_target_pairs={{0,1},{1,0},{2,3},{3,2},{4,5},{5,4},{6,7},{7,6},{8,9},{9,8},{10,11... | collective-permute-start | bytes 122888 | tf_op jit(solution)/shard_map/ppermute | solution.py:237
  4.8 0.5 %inner.1 = (bf16[6,6,32,128]{3,2,1,0:T(8,128)(2,1)S(1)}, f32[288,96]{1,0:T(8,128)S(1)}) custom-call(bf16[4,4,96,128]{3,2,1,0:T(8,128)(2,1)S(1)} %activation.1.act_ref, bf16[4,4,32,128]{3,2,1,0:T(8,128)(2,1)S(1)} %get-tuple-element.16.grad_ref, bf16[4,32,128]{2,1,0:T(8,128)(2,1)S(1)} %collective-permute-done.near_ref), custom_call_target="tpu_custom_call" | custom-call | flops 113246208 | bytes 962560 | tf_op jit(solution)/shard_map/inner/pallas_call | solution.py:256
  5.3 0.9 %collective-permute-done.1.even_ref = bf16[5,32,128]{2,1,0:T(8,128)(2,1)S(1)} collective-permute-done((bf16[5,32,128]{2,1,0:T(8,128)(2,1)S(1)}, bf16[5,32,128]{2,1,0:T(8,128)(2,1)S(1)}, u32[]{:S(2)}, u32[]{:S(2)}) %collective-permute-start.1) | collective-permute-done | bytes 40992 | tf_op jit(solution)/shard_map/ppermute | solution.py:237
  6.2 2.1 %collective-permute-done.2.odd_ref = bf16[5,32,128]{2,1,0:T(8,128)(2,1)S(1)} collective-permute-done((bf16[5,32,128]{2,1,0:T(8,128)(2,1)S(1)}, bf16[5,32,128]{2,1,0:T(8,128)(2,1)S(1)}, u32[]{:S(2)}, u32[]{:S(2)}) %collective-permute-start.2) | collective-permute-done | bytes 40992 | tf_op jit(solution)/shard_map/ppermute | solution.py:237
  8.3 0.3 edges.1
  8.6 2.9 %collective-permute-start.5 = (bf16[10,32,128]{2,1,0:T(8,128)(2,1)S(1)}, bf16[10,32,128]{2,1,0:T(8,128)(2,1)S(1)}, u32[]{:S(2)}, u32[]{:S(2)}) collective-permute-start(bf16[10,32,128]{2,1,0:T(8,128)(2,1)S(1)} %get-tuple-element.25), channel_id=1, source_target_pairs={{0,24},{1,25},{2,26},{3,27},{4,28},{5,29},{6,30},{7,31},{8,16},{9,... | collective-permute-start | bytes 245768 | tf_op jit(solution)/shard_map/ppermute | solution.py:237
  11.6 1.2 %collective-permute-done.3 = f32[112,128]{1,0:T(8,128)S(1)} collective-permute-done((f32[112,128]{1,0:T(8,128)S(1)}, f32[112,128]{1,0:T(8,128)S(1)}, u32[]{:S(2)}, u32[]{:S(2)}) %collective-permute-start.3) | collective-permute-done | bytes 57376 | tf_op jit(solution)/shard_map/ppermute | solution.py:237
  12.8 0.3 collective-permute-start.4
  13.2 1.6 %collective-permute-done.5.far_ref = bf16[10,32,128]{2,1,0:T(8,128)(2,1)S(1)} collective-permute-done((bf16[10,32,128]{2,1,0:T(8,128)(2,1)S(1)}, bf16[10,32,128]{2,1,0:T(8,128)(2,1)S(1)}, u32[]{:S(2)}, u32[]{:S(2)}) %collective-permute-start.5) | collective-permute-done | bytes 81952 | tf_op jit(solution)/shard_map/ppermute | solution.py:237
  14.8 0.4 %across.1 = (f32[112,128]{1,0:T(8,128)S(1)}, f32[112,128]{1,0:T(8,128)S(1)}) custom-call(bf16[4,4,96,128]{3,2,1,0:T(8,128)(2,1)S(1)} %activation.1.act_ref, bf16[6,6,32,128]{3,2,1,0:T(8,128)(2,1)S(1)} %get-tuple-element.24.cells.cells_ref, bf16[10,32,128]{2,1,0:T(8,128)(2,1)S(1)} %collective-permute-done.5.far_ref), custom_call_target="tpu_custom_call" | custom-call | flops 65536 | bytes 884736 | tf_op jit(solution)/shard_map/across/pallas_call | solution.py:256
  15.2 0.5 %collective-permute-start.6 = (f32[112,128]{1,0:T(8,128)S(1)}, f32[112,128]{1,0:T(8,128)S(1)}, u32[]{:S(2)}, u32[]{:S(2)}) collective-permute-start(f32[112,128]{1,0:T(8,128)S(1)} %get-tuple-element.27), channel_id=1, source_target_pairs={{0,8},{1,9},{2,10},{3,11},{4,12},{5,13},{6,14},{7,15},{8,0},{9,1},... | collective-permute-start | bytes 172040 | tf_op jit(solution)/shard_map/ppermute | solution.py:237
  15.6 0.9 %collective-permute-done.4 = f32[112,128]{1,0:T(8,128)S(1)} collective-permute-done((f32[112,128]{1,0:T(8,128)S(1)}, f32[112,128]{1,0:T(8,128)S(1)}, u32[]{:S(2)}, u32[]{:S(2)}) %collective-permute-start.4) | collective-permute-done | bytes 57376 | tf_op jit(solution)/shard_map/ppermute | solution.py:237
  16.7 1.3 %inputs.1 = bf16[32,4,4,128]{3,2,1,0:T(4,128)(2,1)} custom-call(bf16[6,6,32,128]{3,2,1,0:T(8,128)(2,1)S(1)} %get-tuple-element.24.cells.cells_ref, bf16[10,32,128]{2,1,0:T(8,128)(2,1)S(1)} %collective-permute-done.5.far_ref, bf16[3,3,3,32,32]{4,3,2,1,0:T(8,128)(2,1)S(1)} %copy-done), custom_call_target="tpu_custom_call" | custom-call | flops 113246208 | bytes 563200 | tf_op jit(solution)/shard_map/inputs/pallas_call | solution.py:256
  18.0 2.5 %collective-permute-done.7 = f32[112,128]{1,0:T(8,128)S(1)} collective-permute-done((f32[112,128]{1,0:T(8,128)S(1)}, f32[112,128]{1,0:T(8,128)S(1)}, u32[]{:S(2)}, u32[]{:S(2)}) %collective-permute-start.7) | collective-permute-done | bytes 57376 | tf_op jit(solution)/shard_map/ppermute | solution.py:237
  20.5 0.4 %collective-permute-start.8 = (f32[112,128]{1,0:T(8,128)S(1)}, f32[112,128]{1,0:T(8,128)S(1)}, u32[]{:S(2)}, u32[]{:S(2)}) collective-permute-start(f32[112,128]{1,0:T(8,128)S(1)} %add.25), channel_id=1, source_target_pairs={{0,10},{1,11},{2,8},{3,9},{4,14},{5,15},{6,12},{7,13},{8,2},{9,3},... | collective-permute-start | bytes 172040 | tf_op jit(solution)/shard_map/ppermute | solution.py:237
  20.9 3.5 %collective-permute-done.8 = f32[112,128]{1,0:T(8,128)S(1)} collective-permute-done((f32[112,128]{1,0:T(8,128)S(1)}, f32[112,128]{1,0:T(8,128)S(1)}, u32[]{:S(2)}, u32[]{:S(2)}) %collective-permute-start.8) | collective-permute-done | bytes 57376 | tf_op jit(solution)/shard_map/ppermute | solution.py:237
  24.4 0.3 collective-permute-start.9
  24.7 5.9 %collective-permute-done.9 = f32[112,128]{1,0:T(8,128)S(1)} collective-permute-done((f32[112,128]{1,0:T(8,128)S(1)}, f32[112,128]{1,0:T(8,128)S(1)}, u32[]{:S(2)}, u32[]{:S(2)}) %collective-permute-start.9) | collective-permute-done | bytes 57376 | tf_op jit(solution)/shard_map/ppermute | solution.py:237
  30.6 0.5 %collective-permute-start.10 = (f32[112,128]{1,0:T(8,128)S(1)}, f32[112,128]{1,0:T(8,128)S(1)}, u32[]{:S(2)}, u32[]{:S(2)}) collective-permute-start(f32[112,128]{1,0:T(8,128)S(1)} %add.27.half_ref), channel_id=1, source_target_pairs={{0,8},{1,9},{2,10},{3,11},{4,12},{5,13},{6,14},{7,15},{8,0},{9,1},... | collective-permute-start | bytes 172040 | tf_op jit(solution)/shard_map/ppermute | solution.py:237
  31.1 0.8 %finish.2.refs_0_ = f32[3,3,3,32,32]{4,3,2,1,0:T(8,128)} custom-call(f32[112,128]{1,0:T(8,128)S(1)} %add.27.half_ref), custom_call_target="tpu_custom_call" | custom-call | bytes 114688 | tf_op jit(solution)/shard_map/finish/pallas_call | solution.py:344
  32.0 0.8 %finish.3 = f32[3,3,3,32,32]{4,3,2,1,0:T(8,128)} custom-call(f32[112,128]{1,0:T(8,128)S(1)} %collective-permute-done.10.half_ref, f32[3,3,3,32,32]{4,3,2,1,0:T(8,128)} %finish.2.refs_0_), custom_call_target="tpu_custom_call", output_to_operand_aliasing={{}: (1, {})} | custom-call | bytes 114688 | tf_op jit(solution)/shard_map/finish/pallas_call | solution.py:344
  (18 shorter events, 0.7 us)
Async XLA Ops:
  0.6 0.9 %copy-start.1 = (bf16[32,4,4,128]{3,2,1,0:T(4,128)(2,1)S(1)}, bf16[32,4,4,128]{3,2,1,0:T(4,128)(2,1)}, u32[]{:S(2)}) copy-start(bf16[32,4,4,128]{3,2,1,0:T(4,128)(2,1)} %grad_hbm.1) | copy-start | bytes 393220
  1.5 3.1 %copy-start.2 = (bf16[32,4,4,128]{3,2,1,0:T(4,128)(2,1)S(1)}, bf16[32,4,4,128]{3,2,1,0:T(4,128)(2,1)}, u32[]{:S(2)}) copy-start(bf16[32,4,4,128]{3,2,1,0:T(4,128)(2,1)} %act_ref.1) | copy-start | bytes 393220
  1.7 1.6 %collective-permute-start = (bf16[4,32,128]{2,1,0:T(8,128)(2,1)S(1)}, bf16[4,32,128]{2,1,0:T(8,128)(2,1)S(1)}, u32[]{:S(2)}, u32[]{:S(2)}) collective-permute-start(bf16[4,32,128]{2,1,0:T(8,128)(2,1)S(1)} %get-tuple-element.17), channel_id=1, source_target_pairs={{0,8},{1,9},{2,10},{3,11},{4,12},{5,13},{6,14},{7,15},{8,0},{9,1},... | collective-permute-start | bytes 98312 | tf_op jit(solution)/shard_map/ppermute | solution.py:237
  3.3 2.9 %collective-permute-start.1 = (bf16[5,32,128]{2,1,0:T(8,128)(2,1)S(1)}, bf16[5,32,128]{2,1,0:T(8,128)(2,1)S(1)}, u32[]{:S(2)}, u32[]{:S(2)}) collective-permute-start(bf16[5,32,128]{2,1,0:T(8,128)(2,1)S(1)} %get-tuple-element.20), channel_id=1, source_target_pairs={{0,1},{1,0},{2,3},{3,2},{4,5},{5,4},{6,7},{7,6},{8,9},{9,8},{10,11... | collective-permute-start | bytes 122888 | tf_op jit(solution)/shard_map/ppermute | solution.py:237
  4.6 3.8 %collective-permute-start.2 = (bf16[5,32,128]{2,1,0:T(8,128)(2,1)S(1)}, bf16[5,32,128]{2,1,0:T(8,128)(2,1)S(1)}, u32[]{:S(2)}, u32[]{:S(2)}) collective-permute-start(bf16[5,32,128]{2,1,0:T(8,128)(2,1)S(1)} %get-tuple-element.21), channel_id=1, source_target_pairs={{0,8},{1,2},{2,1},{3,4},{4,3},{5,6},{6,5},{7,15},{8,0},{9,10},{10,... | collective-permute-start | bytes 122888 | tf_op jit(solution)/shard_map/ppermute | solution.py:237
  8.6 6.1 %collective-permute-start.5 = (bf16[10,32,128]{2,1,0:T(8,128)(2,1)S(1)}, bf16[10,32,128]{2,1,0:T(8,128)(2,1)S(1)}, u32[]{:S(2)}, u32[]{:S(2)}) collective-permute-start(bf16[10,32,128]{2,1,0:T(8,128)(2,1)S(1)} %get-tuple-element.25), channel_id=1, source_target_pairs={{0,24},{1,25},{2,26},{3,27},{4,28},{5,29},{6,30},{7,31},{8,16},{9,... | collective-permute-start | bytes 245768 | tf_op jit(solution)/shard_map/ppermute | solution.py:237
  11.6 1.2 %collective-permute-start.3 = (f32[112,128]{1,0:T(8,128)S(1)}, f32[112,128]{1,0:T(8,128)S(1)}, u32[]{:S(2)}, u32[]{:S(2)}) collective-permute-start(f32[112,128]{1,0:T(8,128)S(1)} %get-tuple-element.23), channel_id=1, source_target_pairs={{0,8},{1,9},{2,10},{3,11},{4,12},{5,13},{6,14},{7,15},{8,0},{9,1},... | collective-permute-start | bytes 172040 | tf_op jit(solution)/shard_map/ppermute | solution.py:237
  12.8 3.7 %collective-permute-start.4 = (f32[112,128]{1,0:T(8,128)S(1)}, f32[112,128]{1,0:T(8,128)S(1)}, u32[]{:S(2)}, u32[]{:S(2)}) collective-permute-start(f32[112,128]{1,0:T(8,128)S(1)} %add.21), channel_id=1, source_target_pairs={{0,24},{1,25},{2,26},{3,27},{4,28},{5,29},{6,30},{7,31},{8,16},{9,... | collective-permute-start | bytes 172040 | tf_op jit(solution)/shard_map/ppermute | solution.py:237
  15.1 1.5 %copy-start = (bf16[3,3,3,32,32]{4,3,2,1,0:T(8,128)(2,1)S(1)}, bf16[3,3,3,32,32]{4,3,2,1,0:T(8,128)(2,1)}, u32[]{:S(2)}) copy-start(bf16[3,3,3,32,32]{4,3,2,1,0:T(8,128)(2,1)} %kernel_ref.1) | copy-start | bytes 165892
  15.2 1.4 %collective-permute-start.6 = (f32[112,128]{1,0:T(8,128)S(1)}, f32[112,128]{1,0:T(8,128)S(1)}, u32[]{:S(2)}, u32[]{:S(2)}) collective-permute-start(f32[112,128]{1,0:T(8,128)S(1)} %get-tuple-element.27), channel_id=1, source_target_pairs={{0,8},{1,9},{2,10},{3,11},{4,12},{5,13},{6,14},{7,15},{8,0},{9,1},... | collective-permute-start | bytes 172040 | tf_op jit(solution)/shard_map/ppermute | solution.py:237
  16.6 3.9 %collective-permute-start.7 = (f32[112,128]{1,0:T(8,128)S(1)}, f32[112,128]{1,0:T(8,128)S(1)}, u32[]{:S(2)}, u32[]{:S(2)}) collective-permute-start(f32[112,128]{1,0:T(8,128)S(1)} %add_add_fusion), channel_id=1, source_target_pairs={{0,9},{1,8},{2,11},{3,10},{4,13},{5,12},{6,15},{7,14},{8,1},{9,0},... | collective-permute-start | bytes 172040 | tf_op jit(solution)/shard_map/ppermute | solution.py:237
  20.5 3.9 %collective-permute-start.8 = (f32[112,128]{1,0:T(8,128)S(1)}, f32[112,128]{1,0:T(8,128)S(1)}, u32[]{:S(2)}, u32[]{:S(2)}) collective-permute-start(f32[112,128]{1,0:T(8,128)S(1)} %add.25), channel_id=1, source_target_pairs={{0,10},{1,11},{2,8},{3,9},{4,14},{5,15},{6,12},{7,13},{8,2},{9,3},... | collective-permute-start | bytes 172040 | tf_op jit(solution)/shard_map/ppermute | solution.py:237
  24.4 6.2 %collective-permute-start.9 = (f32[112,128]{1,0:T(8,128)S(1)}, f32[112,128]{1,0:T(8,128)S(1)}, u32[]{:S(2)}, u32[]{:S(2)}) collective-permute-start(f32[112,128]{1,0:T(8,128)S(1)} %add.26), channel_id=1, source_target_pairs={{0,12},{1,13},{2,14},{3,15},{4,8},{5,9},{6,10},{7,11},{8,4},{9,5},... | collective-permute-start | bytes 172040 | tf_op jit(solution)/shard_map/ppermute | solution.py:237
  30.6 1.4 %collective-permute-start.10 = (f32[112,128]{1,0:T(8,128)S(1)}, f32[112,128]{1,0:T(8,128)S(1)}, u32[]{:S(2)}, u32[]{:S(2)}) collective-permute-start(f32[112,128]{1,0:T(8,128)S(1)} %add.27.half_ref), channel_id=1, source_target_pairs={{0,8},{1,9},{2,10},{3,11},{4,12},{5,13},{6,14},{7,15},{8,0},{9,1},... | collective-permute-start | bytes 172040 | tf_op jit(solution)/shard_map/ppermute | solution.py:237

commit v4 on v3

--- a/solution.py
+++ b/solution.py
@@ -6,6 +6,7 @@
 from jax.experimental import pallas as pl
 from jax.experimental.pallas import tpu as pltpu
 from jax.sharding import PartitionSpec as P
+
 
 BOTH = ("gx", "gy")
 VMEM = pl.BlockSpec(memory_space=pltpu.VMEM)
@@ -160,7 +161,7 @@
 
 
 def across_body(both, act_ref, cells, far_ref, send_out, keep_out, acc):
-    size_x, size_y, rows3, size_z = act_ref.shape
+    size_x, size_y, rows3, _ = act_ref.shape
     channels = rows3 // 3
     ix = lax.axis_index("gx")
     even = ix % 2 == 0
@@ -250,7 +251,7 @@
             return ix ^ 1, iy
         return ix, (iy + 1 if iy % 2 else iy - 1)
 
-    def call(name, body, out_shape, arrays, scratch=(), flops=0, in_specs=None, limit=16 << 20):
+    def call(body, out_shape, arrays, scratch=(), flops=0, in_specs=None, limit=16 << 20):
         outs = out_shape if isinstance(out_shape, tuple) else (out_shape,)
         nbytes = sum(a.size * a.dtype.itemsize for a in (*arrays, *outs))
         return pl.pallas_call(
@@ -261,11 +262,9 @@
             scratch_shapes=list(scratch),
             compiler_params=params(limit),
             cost_estimate=cost(flops, nbytes),
-            name=name,
         )(*arrays)
 
     grad, near = call(
-        "gradient",
         gradient_body,
         (shape((size_x, size_y, channels, size_z), BF16), shape((size_y, channels, size_z), BF16)),
         (out_grad,),
@@ -278,28 +277,16 @@
     )
     near = permute(near, core)
     face = shape((size_x + 1, channels, size_z), BF16)
-    even, odd = call("faces", faces_body, (face, face), (grad, near))
+    even, odd = call(faces_body, (face, face), (grad, near))
     odd = permute(odd, odd_y)
     even = permute(even, even_y)
-    act = call(
-        "activation",
-        activation_body,
-        shape((size_x, size_y, 3 * channels, size_z), BF16),
-        (activation,),
-    )
+    act = call(activation_body, shape((size_x, size_y, 3 * channels, size_z), BF16), (activation,))
     cells_shape = shape((size_x + 2, size_y + 2, channels, size_z), BF16)
     terms = shape((9 * channels, 3 * channels), F32)
     half = shape((7 * channels // 2, 4 * channels), F32)
     acc = pltpu.VMEM(terms.shape, F32)
-    cells, inner = call(
-        "inner",
-        inner_body,
-        (cells_shape, terms),
-        (act, grad, near),
-        flops=54 * channels * volume,
-    )
+    cells, inner = call(inner_body, (cells_shape, terms), (act, grad, near), flops=54 * channels * volume)
     cells, far, send, total = call(
-        "edges",
         edges_body,
         (cells_shape, shape((2 * size_y + 2, channels, size_z), BF16), half, half),
         (act, cells, inner, even, odd),
@@ -311,7 +298,7 @@
         total = total + permute(send, core)
     far = permute(far, odd_x)
     across = functools.partial(across_body, both)
-    far_send, far_total = call("across", across, (half, half), (act, cells, far), (acc,), flops=volume)
+    far_send, far_total = call(across, (half, half), (act, cells, far), (acc,), flops=volume)
     if both:
         far_total = far_total + permute(far_send, core)
     else:
@@ -323,7 +310,6 @@
     if both:
         total = total + far_total
     grad_input = call(
-        "inputs",
         inputs_body,
         shape(activation.shape, BF16),
         (cells, far, kernel),

time: 32.9 us -> 32.9 us (level)
  no operation moved by 1% of the time
where the time goes in v4:
time: 32.9 us; the launch traced here: 32.8 us
  waiting for transfers between devices  19.6 us (60%)
  starting transfers between devices  7.11 us (22%)
  Pallas kernels  4.37 us (13%)
  local copies, waits for them, and re-layouts  0.91 us (3%)
  between operations  0.73 us (2%)
    ppermute x11, waiting for transfers between devices, permute(): return lax.ppermute(value, BOTH, pairs(counts, partner))  19.6 us
    ppermute x11, starting transfers between devices, permute(): return lax.ppermute(value, BOTH, pairs(counts, partner))  7.11 us
    pallas_call x7, Pallas kernels, call(): pl.pallas_call(body, out_shape=out_shape, in_specs=in_specs or [VMEM] * l...  2.77 us
    pallas_call x2, Pallas kernels, finished(): pl.pallas_call(finish, out_shape=shape(kernel.shape, F32), grid=(1,), in_...  1.59 us
    unnamed x6, local copies, waits for them, and re-layouts  0.91 us
  transfers between devices with their start and end apart: 11, of which 10 were waited for; matrix products, arithmetic and copies ran while one was open for 0% of the time, Pallas kernels for 9%

profile of v4, /device:TPU:25, one launch (start us, length us, event | category | flops | bytes accessed | tf_op | source)
XLA Modules:
  0.0 32.8 jit_solution(5142035352907747576)
XLA Ops:
  0.6 0.9 %copy-done.1 = bf16[32,4,4,128]{3,2,1,0:T(4,128)(2,1)S(1)} copy-done((bf16[32,4,4,128]{3,2,1,0:T(4,128)(2,1)S(1)}, bf16[32,4,4,128]{3,2,1,0:T(4,128)(2,1)}, u32[]{:S(2)}) %copy-start.1) | copy-done | bytes 131096
  1.7 0.7 %collective-permute-start = (bf16[4,32,128]{2,1,0:T(8,128)(2,1)S(1)}, bf16[4,32,128]{2,1,0:T(8,128)(2,1)S(1)}, u32[]{:S(2)}, u32[]{:S(2)}) collective-permute-start(bf16[4,32,128]{2,1,0:T(8,128)(2,1)S(1)} %get-tuple-element.17), channel_id=1, source_target_pairs={{0,8},{1,9},{2,10},{3,11},{4,12},{5,13},{6,14},{7,15},{8,0},{9,1},... | collective-permute-start | bytes 98312 | tf_op jit(solution)/shard_map/ppermute | solution.py:238
  2.5 0.9 %collective-permute-done.near_ref = bf16[4,32,128]{2,1,0:T(8,128)(2,1)S(1)} collective-permute-done((bf16[4,32,128]{2,1,0:T(8,128)(2,1)S(1)}, bf16[4,32,128]{2,1,0:T(8,128)(2,1)S(1)}, u32[]{:S(2)}, u32[]{:S(2)}) %collective-permute-start) | collective-permute-done | bytes 32800 | tf_op jit(solution)/shard_map/ppermute | solution.py:238
  3.3 1.2 %collective-permute-start.1 = (bf16[5,32,128]{2,1,0:T(8,128)(2,1)S(1)}, bf16[5,32,128]{2,1,0:T(8,128)(2,1)S(1)}, u32[]{:S(2)}, u32[]{:S(2)}) collective-permute-start(bf16[5,32,128]{2,1,0:T(8,128)(2,1)S(1)} %get-tuple-element.20), channel_id=1, source_target_pairs={{0,1},{1,0},{2,3},{3,2},{4,5},{5,4},{6,7},{7,6},{8,9},{9,8},{10,11... | collective-permute-start | bytes 122888 | tf_op jit(solution)/shard_map/ppermute | solution.py:238
  4.8 0.5 %shard_map.52 = (bf16[6,6,32,128]{3,2,1,0:T(8,128)(2,1)S(1)}, f32[288,96]{1,0:T(8,128)S(1)}) custom-call(bf16[4,4,96,128]{3,2,1,0:T(8,128)(2,1)S(1)} %shard_map.50.act_ref, bf16[4,4,32,128]{3,2,1,0:T(8,128)(2,1)S(1)} %get-tuple-element.16.grad_ref, bf16[4,32,128]{2,1,0:T(8,128)(2,1)S(1)} %collective-permute-done.near_ref), custom_call_target="tpu_custom_call" | custom-call | flops 113246208 | bytes 962560 | tf_op jit(solution)/shard_map/pallas_call | solution.py:257
  5.3 0.9 %collective-permute-done.1.even_ref = bf16[5,32,128]{2,1,0:T(8,128)(2,1)S(1)} collective-permute-done((bf16[5,32,128]{2,1,0:T(8,128)(2,1)S(1)}, bf16[5,32,128]{2,1,0:T(8,128)(2,1)S(1)}, u32[]{:S(2)}, u32[]{:S(2)}) %collective-permute-start.1) | collective-permute-done | bytes 40992 | tf_op jit(solution)/shard_map/ppermute | solution.py:238
  6.2 2.1 %collective-permute-done.2.odd_ref = bf16[5,32,128]{2,1,0:T(8,128)(2,1)S(1)} collective-permute-done((bf16[5,32,128]{2,1,0:T(8,128)(2,1)S(1)}, bf16[5,32,128]{2,1,0:T(8,128)(2,1)S(1)}, u32[]{:S(2)}, u32[]{:S(2)}) %collective-permute-start.2) | collective-permute-done | bytes 40992 | tf_op jit(solution)/shard_map/ppermute | solution.py:238
  8.3 0.3 shard_map.54
  8.6 2.9 %collective-permute-start.5 = (bf16[10,32,128]{2,1,0:T(8,128)(2,1)S(1)}, bf16[10,32,128]{2,1,0:T(8,128)(2,1)S(1)}, u32[]{:S(2)}, u32[]{:S(2)}) collective-permute-start(bf16[10,32,128]{2,1,0:T(8,128)(2,1)S(1)} %get-tuple-element.25), channel_id=1, source_target_pairs={{0,24},{1,25},{2,26},{3,27},{4,28},{5,29},{6,30},{7,31},{8,16},{9,... | collective-permute-start | bytes 245768 | tf_op jit(solution)/shard_map/ppermute | solution.py:238
  11.6 1.2 %collective-permute-done.3 = f32[112,128]{1,0:T(8,128)S(1)} collective-permute-done((f32[112,128]{1,0:T(8,128)S(1)}, f32[112,128]{1,0:T(8,128)S(1)}, u32[]{:S(2)}, u32[]{:S(2)}) %collective-permute-start.3) | collective-permute-done | bytes 57376 | tf_op jit(solution)/shard_map/ppermute | solution.py:238
  12.8 0.3 collective-permute-start.4
  13.2 1.6 %collective-permute-done.5.far_ref = bf16[10,32,128]{2,1,0:T(8,128)(2,1)S(1)} collective-permute-done((bf16[10,32,128]{2,1,0:T(8,128)(2,1)S(1)}, bf16[10,32,128]{2,1,0:T(8,128)(2,1)S(1)}, u32[]{:S(2)}, u32[]{:S(2)}) %collective-permute-start.5) | collective-permute-done | bytes 81952 | tf_op jit(solution)/shard_map/ppermute | solution.py:238
  14.8 0.4 %shard_map.55 = (f32[112,128]{1,0:T(8,128)S(1)}, f32[112,128]{1,0:T(8,128)S(1)}) custom-call(bf16[4,4,96,128]{3,2,1,0:T(8,128)(2,1)S(1)} %shard_map.50.act_ref, bf16[6,6,32,128]{3,2,1,0:T(8,128)(2,1)S(1)} %get-tuple-element.24.cells.cells_ref, bf16[10,32,128]{2,1,0:T(8,128)(2,1)S(1)} %collective-permute-done.5.far_ref), custom_call_target="tpu_custom_call" | custom-call | flops 65536 | bytes 884736 | tf_op jit(solution)/shard_map/pallas_call | solution.py:257
  15.2 0.5 %collective-permute-start.6 = (f32[112,128]{1,0:T(8,128)S(1)}, f32[112,128]{1,0:T(8,128)S(1)}, u32[]{:S(2)}, u32[]{:S(2)}) collective-permute-start(f32[112,128]{1,0:T(8,128)S(1)} %get-tuple-element.27), channel_id=1, source_target_pairs={{0,8},{1,9},{2,10},{3,11},{4,12},{5,13},{6,14},{7,15},{8,0},{9,1},... | collective-permute-start | bytes 172040 | tf_op jit(solution)/shard_map/ppermute | solution.py:238
  15.6 0.9 %collective-permute-done.4 = f32[112,128]{1,0:T(8,128)S(1)} collective-permute-done((f32[112,128]{1,0:T(8,128)S(1)}, f32[112,128]{1,0:T(8,128)S(1)}, u32[]{:S(2)}, u32[]{:S(2)}) %collective-permute-start.4) | collective-permute-done | bytes 57376 | tf_op jit(solution)/shard_map/ppermute | solution.py:238
  16.7 1.3 %shard_map.56 = bf16[32,4,4,128]{3,2,1,0:T(4,128)(2,1)} custom-call(bf16[6,6,32,128]{3,2,1,0:T(8,128)(2,1)S(1)} %get-tuple-element.24.cells.cells_ref, bf16[10,32,128]{2,1,0:T(8,128)(2,1)S(1)} %collective-permute-done.5.far_ref, bf16[3,3,3,32,32]{4,3,2,1,0:T(8,128)(2,1)S(1)} %copy-done), custom_call_target="tpu_custom_call" | custom-call | flops 113246208 | bytes 563200 | tf_op jit(solution)/shard_map/pallas_call | solution.py:257
  18.0 2.5 %collective-permute-done.7 = f32[112,128]{1,0:T(8,128)S(1)} collective-permute-done((f32[112,128]{1,0:T(8,128)S(1)}, f32[112,128]{1,0:T(8,128)S(1)}, u32[]{:S(2)}, u32[]{:S(2)}) %collective-permute-start.7) | collective-permute-done | bytes 57376 | tf_op jit(solution)/shard_map/ppermute | solution.py:238
  20.5 0.4 %collective-permute-start.8 = (f32[112,128]{1,0:T(8,128)S(1)}, f32[112,128]{1,0:T(8,128)S(1)}, u32[]{:S(2)}, u32[]{:S(2)}) collective-permute-start(f32[112,128]{1,0:T(8,128)S(1)} %add.25), channel_id=1, source_target_pairs={{0,10},{1,11},{2,8},{3,9},{4,14},{5,15},{6,12},{7,13},{8,2},{9,3},... | collective-permute-start | bytes 172040 | tf_op jit(solution)/shard_map/ppermute | solution.py:238
  20.9 3.5 %collective-permute-done.8 = f32[112,128]{1,0:T(8,128)S(1)} collective-permute-done((f32[112,128]{1,0:T(8,128)S(1)}, f32[112,128]{1,0:T(8,128)S(1)}, u32[]{:S(2)}, u32[]{:S(2)}) %collective-permute-start.8) | collective-permute-done | bytes 57376 | tf_op jit(solution)/shard_map/ppermute | solution.py:238
  24.4 0.3 collective-permute-start.9
  24.7 5.9 %collective-permute-done.9 = f32[112,128]{1,0:T(8,128)S(1)} collective-permute-done((f32[112,128]{1,0:T(8,128)S(1)}, f32[112,128]{1,0:T(8,128)S(1)}, u32[]{:S(2)}, u32[]{:S(2)}) %collective-permute-start.9) | collective-permute-done | bytes 57376 | tf_op jit(solution)/shard_map/ppermute | solution.py:238
  30.6 0.5 %collective-permute-start.10 = (f32[112,128]{1,0:T(8,128)S(1)}, f32[112,128]{1,0:T(8,128)S(1)}, u32[]{:S(2)}, u32[]{:S(2)}) collective-permute-start(f32[112,128]{1,0:T(8,128)S(1)} %add.27.half_ref), channel_id=1, source_target_pairs={{0,8},{1,9},{2,10},{3,11},{4,12},{5,13},{6,14},{7,15},{8,0},{9,1},... | collective-permute-start | bytes 172040 | tf_op jit(solution)/shard_map/ppermute | solution.py:238
  31.1 0.8 %finish.2.refs_0_ = f32[3,3,3,32,32]{4,3,2,1,0:T(8,128)} custom-call(f32[112,128]{1,0:T(8,128)S(1)} %add.27.half_ref), custom_call_target="tpu_custom_call" | custom-call | bytes 114688 | tf_op jit(solution)/shard_map/finish/pallas_call | solution.py:330
  32.0 0.8 %finish.3 = f32[3,3,3,32,32]{4,3,2,1,0:T(8,128)} custom-call(f32[112,128]{1,0:T(8,128)S(1)} %collective-permute-done.10.half_ref, f32[3,3,3,32,32]{4,3,2,1,0:T(8,128)} %finish.2.refs_0_), custom_call_target="tpu_custom_call", output_to_operand_aliasing={{}: (1, {})} | custom-call | bytes 114688 | tf_op jit(solution)/shard_map/finish/pallas_call | solution.py:330
  (18 shorter events, 0.7 us)
Async XLA Ops:
  0.6 0.9 %copy-start.1 = (bf16[32,4,4,128]{3,2,1,0:T(4,128)(2,1)S(1)}, bf16[32,4,4,128]{3,2,1,0:T(4,128)(2,1)}, u32[]{:S(2)}) copy-start(bf16[32,4,4,128]{3,2,1,0:T(4,128)(2,1)} %grad_hbm.1) | copy-start | bytes 393220
  1.5 3.1 %copy-start.2 = (bf16[32,4,4,128]{3,2,1,0:T(4,128)(2,1)S(1)}, bf16[32,4,4,128]{3,2,1,0:T(4,128)(2,1)}, u32[]{:S(2)}) copy-start(bf16[32,4,4,128]{3,2,1,0:T(4,128)(2,1)} %act_ref.1) | copy-start | bytes 393220
  1.7 1.6 %collective-permute-start = (bf16[4,32,128]{2,1,0:T(8,128)(2,1)S(1)}, bf16[4,32,128]{2,1,0:T(8,128)(2,1)S(1)}, u32[]{:S(2)}, u32[]{:S(2)}) collective-permute-start(bf16[4,32,128]{2,1,0:T(8,128)(2,1)S(1)} %get-tuple-element.17), channel_id=1, source_target_pairs={{0,8},{1,9},{2,10},{3,11},{4,12},{5,13},{6,14},{7,15},{8,0},{9,1},... | collective-permute-start | bytes 98312 | tf_op jit(solution)/shard_map/ppermute | solution.py:238
  3.3 2.9 %collective-permute-start.1 = (bf16[5,32,128]{2,1,0:T(8,128)(2,1)S(1)}, bf16[5,32,128]{2,1,0:T(8,128)(2,1)S(1)}, u32[]{:S(2)}, u32[]{:S(2)}) collective-permute-start(bf16[5,32,128]{2,1,0:T(8,128)(2,1)S(1)} %get-tuple-element.20), channel_id=1, source_target_pairs={{0,1},{1,0},{2,3},{3,2},{4,5},{5,4},{6,7},{7,6},{8,9},{9,8},{10,11... | collective-permute-start | bytes 122888 | tf_op jit(solution)/shard_map/ppermute | solution.py:238
  4.6 3.8 %collective-permute-start.2 = (bf16[5,32,128]{2,1,0:T(8,128)(2,1)S(1)}, bf16[5,32,128]{2,1,0:T(8,128)(2,1)S(1)}, u32[]{:S(2)}, u32[]{:S(2)}) collective-permute-start(bf16[5,32,128]{2,1,0:T(8,128)(2,1)S(1)} %get-tuple-element.21), channel_id=1, source_target_pairs={{0,8},{1,2},{2,1},{3,4},{4,3},{5,6},{6,5},{7,15},{8,0},{9,10},{10,... | collective-permute-start | bytes 122888 | tf_op jit(solution)/shard_map/ppermute | solution.py:238
  8.6 6.1 %collective-permute-start.5 = (bf16[10,32,128]{2,1,0:T(8,128)(2,1)S(1)}, bf16[10,32,128]{2,1,0:T(8,128)(2,1)S(1)}, u32[]{:S(2)}, u32[]{:S(2)}) collective-permute-start(bf16[10,32,128]{2,1,0:T(8,128)(2,1)S(1)} %get-tuple-element.25), channel_id=1, source_target_pairs={{0,24},{1,25},{2,26},{3,27},{4,28},{5,29},{6,30},{7,31},{8,16},{9,... | collective-permute-start | bytes 245768 | tf_op jit(solution)/shard_map/ppermute | solution.py:238
  11.6 1.2 %collective-permute-start.3 = (f32[112,128]{1,0:T(8,128)S(1)}, f32[112,128]{1,0:T(8,128)S(1)}, u32[]{:S(2)}, u32[]{:S(2)}) collective-permute-start(f32[112,128]{1,0:T(8,128)S(1)} %get-tuple-element.23), channel_id=1, source_target_pairs={{0,8},{1,9},{2,10},{3,11},{4,12},{5,13},{6,14},{7,15},{8,0},{9,1},... | collective-permute-start | bytes 172040 | tf_op jit(solution)/shard_map/ppermute | solution.py:238
  12.8 3.7 %collective-permute-start.4 = (f32[112,128]{1,0:T(8,128)S(1)}, f32[112,128]{1,0:T(8,128)S(1)}, u32[]{:S(2)}, u32[]{:S(2)}) collective-permute-start(f32[112,128]{1,0:T(8,128)S(1)} %add.21), channel_id=1, source_target_pairs={{0,24},{1,25},{2,26},{3,27},{4,28},{5,29},{6,30},{7,31},{8,16},{9,... | collective-permute-start | bytes 172040 | tf_op jit(solution)/shard_map/ppermute | solution.py:238
  15.1 1.5 %copy-start = (bf16[3,3,3,32,32]{4,3,2,1,0:T(8,128)(2,1)S(1)}, bf16[3,3,3,32,32]{4,3,2,1,0:T(8,128)(2,1)}, u32[]{:S(2)}) copy-start(bf16[3,3,3,32,32]{4,3,2,1,0:T(8,128)(2,1)} %kernel_ref.1) | copy-start | bytes 165892
  15.2 1.4 %collective-permute-start.6 = (f32[112,128]{1,0:T(8,128)S(1)}, f32[112,128]{1,0:T(8,128)S(1)}, u32[]{:S(2)}, u32[]{:S(2)}) collective-permute-start(f32[112,128]{1,0:T(8,128)S(1)} %get-tuple-element.27), channel_id=1, source_target_pairs={{0,8},{1,9},{2,10},{3,11},{4,12},{5,13},{6,14},{7,15},{8,0},{9,1},... | collective-permute-start | bytes 172040 | tf_op jit(solution)/shard_map/ppermute | solution.py:238
  16.6 3.9 %collective-permute-start.7 = (f32[112,128]{1,0:T(8,128)S(1)}, f32[112,128]{1,0:T(8,128)S(1)}, u32[]{:S(2)}, u32[]{:S(2)}) collective-permute-start(f32[112,128]{1,0:T(8,128)S(1)} %add_add_fusion), channel_id=1, source_target_pairs={{0,9},{1,8},{2,11},{3,10},{4,13},{5,12},{6,15},{7,14},{8,1},{9,0},... | collective-permute-start | bytes 172040 | tf_op jit(solution)/shard_map/ppermute | solution.py:238
  20.5 3.9 %collective-permute-start.8 = (f32[112,128]{1,0:T(8,128)S(1)}, f32[112,128]{1,0:T(8,128)S(1)}, u32[]{:S(2)}, u32[]{:S(2)}) collective-permute-start(f32[112,128]{1,0:T(8,128)S(1)} %add.25), channel_id=1, source_target_pairs={{0,10},{1,11},{2,8},{3,9},{4,14},{5,15},{6,12},{7,13},{8,2},{9,3},... | collective-permute-start | bytes 172040 | tf_op jit(solution)/shard_map/ppermute | solution.py:238
  24.4 6.2 %collective-permute-start.9 = (f32[112,128]{1,0:T(8,128)S(1)}, f32[112,128]{1,0:T(8,128)S(1)}, u32[]{:S(2)}, u32[]{:S(2)}) collective-permute-start(f32[112,128]{1,0:T(8,128)S(1)} %add.26), channel_id=1, source_target_pairs={{0,12},{1,13},{2,14},{3,15},{4,8},{5,9},{6,10},{7,11},{8,4},{9,5},... | collective-permute-start | bytes 172040 | tf_op jit(solution)/shard_map/ppermute | solution.py:238
  30.6 1.4 %collective-permute-start.10 = (f32[112,128]{1,0:T(8,128)S(1)}, f32[112,128]{1,0:T(8,128)S(1)}, u32[]{:S(2)}, u32[]{:S(2)}) collective-permute-start(f32[112,128]{1,0:T(8,128)S(1)} %add.27.half_ref), channel_id=1, source_target_pairs={{0,8},{1,9},{2,10},{3,11},{4,12},{5,13},{6,14},{7,15},{8,0},{9,1},... | collective-permute-start | bytes 172040 | tf_op jit(solution)/shard_map/ppermute | solution.py:238
